TPU v7x, 256 devices: a whole 4x4x8 slice. The times are simulated.
256 devices in a mesh: row: 64 (over z_hi, y, x, core), col: 4 (over z_lo).
Axes of the slice: x: 4, y: 4, z: 8 (z_hi: 2, z_lo: 4; z = z_hi * 4 + z_lo), core: 2. Of those that a mesh axis runs over, the one named last changes fastest.
Arguments:
- node_features: bfloat16 [262144, 256], P(('row', 'col')), may hold values from -6 to 6
- tile_cols: int32 [4096, 8], P(('row', 'col')), may hold values from 0 to 4095, as said below
- tile_weights: int32 [4096, 64, 512], P(('row', 'col')), may hold values from 0 to 7
- w_self: bfloat16 [256, 1024], replicated, may hold values from -0.375 to 0.375
- w_neigh: bfloat16 [256, 1024], replicated, may hold values from -0.375 to 0.375
- bias_hidden: float32 [1024], replicated, may hold values from -3 to 3
- w_out: bfloat16 [1024, 256], replicated, may hold values from -0.1875 to 0.1875
- bias_out: float32 [256], replicated, may hold values from -3 to 3
- cotangent: bfloat16 [262144, 256], P(('row', 'col')), may hold values from -6 to 6
Outputs:
- embed: bfloat16 [262144, 256], P(('row', 'col'))
- grad_features: bfloat16 [262144, 256], P(('row', 'col'))
- grad_w_self: float32 [256, 1024], replicated
- grad_w_neigh: float32 [256, 1024], replicated
- grad_bias_hidden: float32 [1024], replicated
- grad_w_out: float32 [1024, 256], replicated
- grad_bias_out: float32 [256], replicated
Inputs may be any that keep to these rules, and one draw needn't show every extreme that they name: `tile_cols`: the first tile of block row b is its diagonal block b. The second lies exactly 16 block rows before or after b (the side drawn for each row), clipped to the graph. Every tile's block column differs from its block row by at most 16.
All inputs are finite; a program needn't handle non-finite values.
Results may differ from a plain program's by a relative error of at most 0.0071.
Values may be sent and summed in bfloat16 or wider, within the bound.
A program may use at most 128 MiB of HBM per device.

v0:
```python
import math

import jax
import jax.numpy as jnp
from jax import lax
from jax.sharding import PartitionSpec as P


def extended(block, sides, width):
    for axis, dim in sides:
        count = lax.axis_size(axis)
        forward = [(i, i + 1) for i in range(count - 1)]
        backward = [(target, source) for source, target in forward]
        low = lax.ppermute(
            lax.slice_in_dim(block, block.shape[dim] - width, None, axis=dim), axis, forward
        )
        high = lax.ppermute(lax.slice_in_dim(block, 0, width, axis=dim), axis, backward)
        block = jnp.concatenate([low, block, high], axis=dim)
    return block


def gelu_tanh(values):
    return jax.nn.gelu(values, approximate=True)


def reduce_grads(partials):
    return lax.psum(
        (partials[0], partials[1], partials[2], partials[3], partials[4]), ("row", "col")
    )


def adjoint_part(adjacency, d_aggregate, local_idx, block_rows, tile_size, per_row, width):
    rows_here = block_rows * tile_size
    spread = jnp.einsum(
        "bij,bif->bjf",
        adjacency,
        d_aggregate.reshape(block_rows, tile_size, width),
        preferred_element_type=jnp.float32,
    )
    spread = spread.reshape(block_rows * per_row, tile_size, width)
    spread_sum = jnp.zeros((3 * block_rows, tile_size, width), jnp.float32)
    spread_sum = spread_sum.at[local_idx.reshape(-1)].add(spread)
    spread_sum = spread_sum.reshape(3 * rows_here, width)
    outer_parts = jnp.concatenate([spread_sum[:rows_here], spread_sum[2 * rows_here :]], axis=0)
    padded = extended(outer_parts, ((("row", "col"), 0),), rows_here)
    return spread_sum[rows_here : 2 * rows_here] + padded[:rows_here] + padded[3 * rows_here :]


def local(
    node_features, tile_cols, tile_weights, w_self, w_neigh, bias_hidden, w_out, bias_out, cotangent
):
    rows_here = node_features.shape[0]
    width = node_features.shape[1]
    tile_size = tile_weights.shape[1]
    per_row = tile_cols.shape[1]
    block_rows = rows_here // tile_size
    devices_all = lax.axis_size(("row", "col"))
    tile_scale = 0.25 / math.sqrt(per_row * tile_size)
    grad_scale = 1.0 / math.sqrt(rows_here * devices_all)
    window = extended(node_features, ((("row", "col"), 0),), rows_here)
    first_block = lax.axis_index(("row", "col")) * block_rows - block_rows
    local_idx = tile_cols - first_block
    all_blocks = window.reshape(3 * block_rows, tile_size, width)
    gathered = all_blocks[local_idx].reshape(block_rows, per_row * tile_size, width)
    adjacency = (tile_weights.astype(jnp.float32) * tile_scale).astype(jnp.bfloat16)
    aggregate = jnp.einsum("bij,bjf->bif", adjacency, gathered, preferred_element_type=jnp.float32)
    aggregate = aggregate.reshape(rows_here, width).astype(jnp.bfloat16)
    preact = (
        jnp.dot(node_features, w_self, preferred_element_type=jnp.float32)
        + jnp.dot(aggregate, w_neigh, preferred_element_type=jnp.float32)
        + bias_hidden
    )
    activated, pullback = jax.vjp(gelu_tanh, preact)
    hidden = activated.astype(jnp.bfloat16)
    embed = (jnp.dot(hidden, w_out, preferred_element_type=jnp.float32) + bias_out).astype(
        jnp.bfloat16
    )
    d_act = jnp.dot(cotangent, w_out.T, preferred_element_type=jnp.float32)
    d_hidden = pullback(d_act)[0].astype(jnp.bfloat16)
    partials = (
        jnp.dot(node_features.T, d_hidden, preferred_element_type=jnp.float32),
        jnp.dot(aggregate.T, d_hidden, preferred_element_type=jnp.float32),
        jnp.sum(d_hidden.astype(jnp.float32), axis=0),
        jnp.dot(hidden.T, cotangent, preferred_element_type=jnp.float32),
        jnp.sum(cotangent.astype(jnp.float32), axis=0),
    )
    d_aggregate = jnp.dot(d_hidden, w_neigh.T, preferred_element_type=jnp.float32).astype(
        jnp.bfloat16
    )
    d_self = jnp.dot(d_hidden, w_self.T, preferred_element_type=jnp.float32)
    rim_total = adjoint_part(
        adjacency, d_aggregate, local_idx, block_rows, tile_size, per_row, width
    )
    reduced = reduce_grads(partials)
    grad_features = (d_self + rim_total).astype(jnp.bfloat16)
    return (
        embed,
        grad_features,
        reduced[0] * grad_scale,
        reduced[1] * grad_scale,
        reduced[2] * grad_scale,
        reduced[3] * grad_scale,
        reduced[4] * grad_scale,
    )


def solution(mesh):
    in_specs = (
        P(("row", "col"), None),
        P(("row", "col"), None),
        P(("row", "col"), None, None),
        P(),
        P(),
        P(),
        P(),
        P(),
        P(("row", "col"), None),
    )
    out_specs = (P(("row", "col"), None), P(("row", "col"), None), P(), P(), P(), P(), P())
    return jax.shard_map(local, mesh=mesh, in_specs=in_specs, out_specs=out_specs, check_vma=False)
```

profile of v0, /device:TPU:1, one launch (start us, length us, event | category | flops | bytes accessed | tf_op | source)
XLA Modules:
  0.0 388.8 jit_solution(17411679388916935601)
XLA Ops:
  7.2 0.0 copy-start
  7.2 0.0 all-reduce.4.cloned.1.call-start
  7.2 7.8 %collective-permute-start.1 = (bf16[1024,256]{1,0:T(8,128)(2,1)}, bf16[1024,256]{1,0:T(8,128)(2,1)S(1)}, u32[]{:S(2)}, u32[]{:S(2)}) collective-permute-start(bf16[1024,256]{1,0:T(8,128)(2,1)} %param.9), channel_id=1, source_target_pairs={{1,0},{2,1},{3,2},{4,3},{5,4},{6,5},{7,6},{8,7},{9,8},{10,9},{11,1... | collective-permute-start | bytes 1572872 | tf_op jit(solution)/shard_map/ppermute | solution.py:17
  15.0 1.9 collective-permute-start
  16.9 0.7 compare_select_fusion
  17.6 0.1 copy.22
  17.7 0.1 reshape.67
  17.8 0.1 copy.21
  17.9 0.1 reshape.72
  18.0 0.0 copy-start.4
  18.0 3.9 %fusion.16 = f32[1024,1024]{1,0:T(8,128)} fusion(bf16[1024,256]{1,0:T(8,128)(2,1)} %param.9, bf16[256,1024]{1,0:T(8,128)(2,1)} %param.12), kind=kOutput, calls=%fused_computation.40 | convolution fusion | flops 536870912 | bytes 5242880 | tf_op jit(solution)/shard_map/dot_general | solution.py:69
  21.9 3.5 collective-permute-done.1
  25.4 12.7 %collective-permute-done = bf16[1024,256]{1,0:T(8,128)(2,1)} collective-permute-done((bf16[1024,256]{1,0:T(8,128)(2,1)}, bf16[1024,256]{1,0:T(8,128)(2,1)}, u32[]{:S(2)}, u32[]{:S(2)}) %collective-permute-start) | collective-permute-done | bytes 524320 | tf_op jit(solution)/shard_map/ppermute | solution.py:14
  38.2 0.0 copy-done.4
  38.2 1.1 pad_maximum_fusion
  39.3 2.8 gather_fusion
  42.1 3.7 convolution_convert_fusion
  45.9 0.3 copy-done.1
  46.1 2.0 multiply_convert_fusion
  48.1 3.4 convert_reduce_fusion
  51.5 0.7 convolution_convert_fusion.1
  52.3 0.0 copy-start.2
  52.3 1.7 convolution_bitcast_fusion
  54.0 1.9 fusion.17
  55.9 0.0 copy-done.2
  55.9 4.5 %fusion.11 = f32[16,512,256]{2,1,0:T(8,128)} fusion(bf16[16,64,256]{2,1,0:T(8,128)(2,1)S(1)} %bitcast.44, s32[16,64,512]{2,1,0:T(8,128)S(1)} %copy-done.2), kind=kOutput, calls=%fused_computation.29 | convolution fusion | flops 270008320 | bytes 11010048 | tf_op jit(solution)/shard_map/bij,bif->bjf/dot_general | solution.py:34
  60.4 1.7 fusion.18
  62.1 2.1 broadcast_in_dim.10
  64.2 26.4 %scatter_fusion = f32[48,64,256]{2,1,0:T(8,128)} fusion(f32[48,64,256]{2,1,0:T(8,128)} %broadcast_in_dim.10, s32[128]{0:T(128)S(1)} %fusion.12, f32[128,64,256]{2,1,0:T(8,128)} %bitcast.39), kind=kCustom, calls=%fused_computation.1 | custom fusion | flops 2097152 | bytes 25166336 | tf_op jit(solution)/shard_map/scatter-add | solution.py:42
  90.6 0.0 all-reduce.4.cloned.1.call-update
  90.6 0.0 copy-start.7
  90.6 0.0 copy-start.10
  90.6 3.7 fusion.15
  94.3 2.0 collective-permute-start.3
  96.4 3.4 collective-permute-start.2
  99.8 0.2 convert_reduce_fusion.1
  99.9 100.2 %all-reduce = (f32[1024]{0:T(1024)S(1)}, f32[256]{0:T(256)S(1)}) all-reduce(f32[1024]{0:T(1024)S(1)} %get-tuple-element.33, f32[256]{0:T(256)S(1)} %convert_reduce_fusion.1), channel_id=1, replica_groups=mesh['row'=64,'col'=4] {'row','col'}, use_global_device_ids=true, to_apply=%region_4.0 | all-reduce | flops 1280 | bytes 10240 | tf_op jit(solution)/shard_map/psum | solution.py:27
  200.1 0.6 broadcast_multiply_fusion.4
  200.7 0.6 broadcast_multiply_fusion.3
  201.3 3.2 fusion.7
  204.5 0.0 collective-permute-done.3
  204.5 0.0 collective-permute-done.2
  204.5 3.1 fusion.10
  207.6 167.8 %all-reduce.4.cloned.1.call-done = (f32[256,1024]{0,1:T(8,128)}, f32[256,1024]{0,1:T(8,128)}, f32[1024,256]{1,0:T(8,128)}) async-done(((f32[256,1024]{0,1:T(8,128)}, f32[256,1024]{0,1:T(8,128)}, f32[1024,256]{1,0:T(8,128)}), (f32[256,1024]{0,1:T(8,128)}, f32[256,1024]{0,1:T(8,128)}, f32[1024,256]{1,0:T(8,128)})) %all-reduce.4.cloned.1.call-update) | async-done | bytes 3145744 | tf_op jit(solution)/shard_map/psum | solution.py:27
  375.4 1.7 broadcast_multiply_fusion.1
  377.0 1.3 copy.24
  378.4 1.3 copy.25
  379.7 2.3 broadcast_multiply_fusion
  (18 shorter events, 0.0 us)
Async XLA Ops:
  7.2 38.7 %copy-start = (bf16[256,1024]{1,0:T(8,128)(2,1)S(1)}, bf16[256,1024]{1,0:T(8,128)(2,1)}, u32[]{:S(2)}) copy-start(bf16[256,1024]{1,0:T(8,128)(2,1)} %param.13) | copy-start | bytes 1572868
  7.2 368.2 %all-reduce.4.cloned.1.call-start = ((), (), s32[]{:S(2)}) async-start(), calls=%async_computation | async-start | bytes 6291456 | tf_op jit(solution)/shard_map/psum | solution.py:27
  7.2 18.2 %collective-permute-start.1 = (bf16[1024,256]{1,0:T(8,128)(2,1)}, bf16[1024,256]{1,0:T(8,128)(2,1)S(1)}, u32[]{:S(2)}, u32[]{:S(2)}) collective-permute-start(bf16[1024,256]{1,0:T(8,128)(2,1)} %param.9), channel_id=1, source_target_pairs={{1,0},{2,1},{3,2},{4,3},{5,4},{6,5},{7,6},{8,7},{9,8},{10,9},{11,1... | collective-permute-start | bytes 1572872 | tf_op jit(solution)/shard_map/ppermute | solution.py:17
  15.0 23.2 %collective-permute-start = (bf16[1024,256]{1,0:T(8,128)(2,1)}, bf16[1024,256]{1,0:T(8,128)(2,1)}, u32[]{:S(2)}, u32[]{:S(2)}) collective-permute-start(bf16[1024,256]{1,0:T(8,128)(2,1)} %param.9), channel_id=1, source_target_pairs={{0,1},{1,2},{2,3},{3,4},{4,5},{5,6},{6,7},{7,8},{8,9},{9,10},{10,1... | collective-permute-start | bytes 1572872 | tf_op jit(solution)/shard_map/ppermute | solution.py:14
  18.0 20.2 %copy-start.4 = (bf16[1024,256]{1,0:T(8,128)(2,1)S(1)}, bf16[1024,256]{1,0:T(8,128)(2,1)}, u32[]{:S(2)}) copy-start(bf16[1024,256]{1,0:T(8,128)(2,1)} %param.9) | copy-start | bytes 1572868
  42.1 4.0 %copy-start.1 = (f32[1024,1024]{1,0:T(8,128)S(1)}, f32[1024,1024]{1,0:T(8,128)}, u32[]{:S(2)}) copy-start(f32[1024,1024]{1,0:T(8,128)} %fusion.16) | copy-start | bytes 12582916
  42.1 4.0 %copy-start.9 = (f32[1024]{0:T(1024)S(1)}, f32[1024]{0:T(1024)}, u32[]{:S(2)}) copy-start(f32[1024]{0:T(1024)} %param.14) | copy-start | bytes 12292
  46.1 2.0 copy-start.6
  46.1 2.0 copy-start.8
  48.1 12.3 %copy-start.11 = (bf16[1024,1024]{1,0:T(8,128)(2,1)}, bf16[1024,1024]{1,0:T(8,128)(2,1)S(1)}, u32[]{:S(2)}) copy-start(bf16[1024,1024]{1,0:T(8,128)(2,1)S(1)} %get-tuple-element.31) | copy-start | bytes 6291460
  52.3 3.7 copy-start.2
  90.6 9.1 %copy-start.7 = (bf16[1024,256]{1,0:T(8,128)(2,1)S(1)}, bf16[1024,256]{1,0:T(8,128)(2,1)}, u32[]{:S(2)}) copy-start(bf16[1024,256]{1,0:T(8,128)(2,1)} %param.17) | copy-start | bytes 1572868
  90.6 110.6 %copy-start.10 = (f32[256]{0:T(256)S(1)}, f32[256]{0:T(256)}, u32[]{:S(2)}) copy-start(f32[256]{0:T(256)} %param.16) | copy-start | bytes 3076
  94.3 110.1 %copy-start.5 = (bf16[256,1024]{1,0:T(8,128)(2,1)S(1)}, bf16[256,1024]{1,0:T(8,128)(2,1)}, u32[]{:S(2)}) copy-start(bf16[256,1024]{1,0:T(8,128)(2,1)} %param.12) | copy-start | bytes 1572868
  94.3 110.1 %collective-permute-start.3 = (f32[1024,256]{1,0:T(8,128)}, f32[1024,256]{1,0:T(8,128)}, u32[]{:S(2)}, u32[]{:S(2)}) collective-permute-start(f32[1024,256]{1,0:T(8,128)} %bitcast.8), channel_id=1, source_target_pairs={{1,0},{2,1},{3,2},{4,3},{5,4},{6,5},{7,6},{8,7},{9,8},{10,9},{11,1... | collective-permute-start | bytes 3145736 | tf_op jit(solution)/shard_map/ppermute | solution.py:17
  96.4 108.1 %collective-permute-start.2 = (f32[1024,256]{1,0:T(8,128)}, f32[1024,256]{1,0:T(8,128)}, u32[]{:S(2)}, u32[]{:S(2)}) collective-permute-start(f32[1024,256]{1,0:T(8,128)} %bitcast.7), channel_id=1, source_target_pairs={{0,1},{1,2},{2,3},{3,4},{4,5},{5,6},{6,7},{7,8},{8,9},{9,10},{10,1... | collective-permute-start | bytes 3145736 | tf_op jit(solution)/shard_map/ppermute | solution.py:14
  200.1 4.4 %copy-start.3 = (f32[16,64,256]{2,1,0:T(8,128)S(1)}, f32[16,64,256]{2,1,0:T(8,128)}, u32[]{:S(2)}) copy-start(f32[16,64,256]{2,1,0:T(8,128)} %get-tuple-element.28) | copy-start | bytes 3145732
Sparse Core Ops, SparseCore 0:
  90.7 284.5 all-reduce.3
where the time goes:
time: 390 us; the launch traced here: 389 us
  waiting for transfers between devices  184 us (47%)
  blocking collectives  100 us (26%)
  other arithmetic  33.5 us (9%)
  matrix products  29.9 us (8%)
  starting transfers between devices  15.1 us (4%)
  between operations  14.2 us (4%)
  local copies, waits for them, and re-layouts  11.8 us (3%)
    psum x1, waiting for transfers between devices, reduce_grads(): lax.psum((partials[0], partials[1], partials[2], partials[3], partials[4]...  168 us
    psum x1, blocking collectives, reduce_grads(): lax.psum((partials[0], partials[1], partials[2], partials[3], partials[4]...  100 us
    scatter-add x1, other arithmetic, adjoint_part(): spread_sum = spread_sum.at[local_idx.reshape(-1)].add(spread)  26.4 us
    ppermute x2, waiting for transfers between devices, extended(): lax.ppermute(lax.slice_in_dim(block, block.shape[dim] - width, None, axis...  12.7 us
    ppermute x2, starting transfers between devices, extended(): lax.ppermute(lax.slice_in_dim(block, 0, width, axis=dim), axis, backward)  9.82 us
  transfers between devices with their start and end apart: 5, of which 3 were waited for; matrix products, arithmetic and copies ran while one was open for 4% of the time, Pallas kernels for 0%

commit v1 on v0

--- a/solution.py
+++ b/solution.py
@@ -1,9 +1,204 @@
-import math
-
-import jax
-import jax.numpy as jnp
+import functools, math
+import jax, jax.numpy as jnp
 from jax import lax
+from jax.experimental import pallas as pl
+from jax.experimental.pallas import tpu as pltpu
 from jax.sharding import PartitionSpec as P
+
+MESH = pl.DeviceIdType.MESH
+BF, F32 = jnp.bfloat16, jnp.float32
+
+
+def coords():
+    row, z_lo = lax.axis_index("row"), lax.axis_index("col")
+    core = row % 2
+    x = (row // 2) % 4
+    y = (row // 8) % 4
+    z = (row // 32) * 4 + z_lo
+    return row, z_lo, core, x, y, z
+
+
+def partners():
+    row, z_lo, core, x, y, z = coords()
+    sibling = [(row + 1 - 2 * core, z_lo, 1 - core)]
+    xs = [(row + ((x + d) % 4 - x) * 2, z_lo, (x + d) % 4) for d in (2, 1, 3)]
+    ys = [(row + ((y + d) % 4 - y) * 8, z_lo, (y + d) % 4) for d in (2, 1, 3)]
+    zs = []
+    for d in (4, 3, 5, 2, 6, 1, 7):
+        k = (z + d) % 8
+        zs.append((row + (k // 4 - z // 4) * 32, k % 4, k))
+    return sibling, xs, ys, zs
+
+
+def remote(src, dst, send, recv, dev):
+    return pltpu.make_async_remote_copy(
+        src_ref=src, dst_ref=dst, send_sem=send, recv_sem=recv,
+        device_id=(dev[0], dev[1]), device_id_type=MESH)
+
+
+def reduce_all(g, bias, gout, bout, rc, s1, r1, t1, r2, zin, rz, zc, zfull, bc, bx, by, bz,
+               send, recv):
+    row, z_lo, core, x, y, z = coords()
+    sibling, xs, ys, zs = partners()
+    A, B = 384, 96
+    sent = []
+    nsend = [0]
+
+    def go(src, dst, rsem, dev):
+        c = remote(src, dst, send.at[nsend[0]], recv.at[rsem], dev)
+        nsend[0] += 1
+        c.start()
+        sent.append(c)
+
+    def land(dst, rsem):
+        remote(dst, dst, send.at[0], recv.at[rsem], sibling[0]).wait_recv()
+
+    mine = pl.ds(pl.multiple_of(core * 512, 512), 512)
+    other = pl.ds(pl.multiple_of((1 - core) * 512, 512), 512)
+    go(g.at[:, other], rc, 0, sibling[0])
+    go(bias, bc, 1, sibling[0])
+    land(rc, 0)
+    land(bc, 1)
+
+    @pl.loop(0, 8)
+    def _(i):
+        rows = pl.ds(pl.multiple_of(i * 96, 96), 96)
+        s1[rows, :] = (g[rows, mine].astype(F32) + rc[rows, :].astype(F32)).astype(BF)
+
+    b1 = bias[...] + bc[...]
+    bx[x] = b1
+    base = 2
+    for h, (line, me) in enumerate(((xs, x), (ys, y))):
+        for dev in line:
+            j = dev[2]
+            rows = pl.ds(pl.multiple_of(h * A + j * B, B), B)
+            go(s1.at[rows, :], r1.at[h, me], base + h * 4 + me, dev)
+    for dev in xs:
+        go(bx.at[x], bx.at[x], base + 8 + x, dev)
+    for h, (line, me) in enumerate(((xs, x), (ys, y))):
+        for dev in line:
+            land(r1.at[h, dev[2]], base + h * 4 + dev[2])
+        own = pl.ds(pl.multiple_of(h * A + me * B, B), B)
+        total = s1[own, :].astype(F32)
+        for dev in line:
+            total = total + r1[h, dev[2]].astype(F32)
+        t1[h] = total.astype(BF)
+    for dev in xs:
+        land(bx.at[dev[2]], base + 8 + dev[2])
+    by[y] = bx[0] + bx[1] + bx[2] + bx[3]
+    base = 14
+    for h, (line, me) in enumerate(((ys, y), (xs, x))):
+        for dev in line:
+            lanes = pl.ds(pl.multiple_of(dev[2] * 128, 128), 128)
+            go(t1.at[h, :, lanes], r2.at[h, me], base + h * 4 + me, dev)
+    for dev in ys:
+        go(by.at[y], by.at[y], base + 8 + y, dev)
+    for h, (line, me) in enumerate(((ys, y), (xs, x))):
+        for dev in line:
+            land(r2.at[h, dev[2]], base + h * 4 + dev[2])
+        total = t1[h, :, pl.ds(pl.multiple_of(me * 128, 128), 128)].astype(F32)
+        for dev in line:
+            total = total + r2[h, dev[2]].astype(F32)
+        zin[h * 4 : h * 4 + 4] = total.reshape(4, 24, 128)
+    for dev in ys:
+        land(by.at[dev[2]], base + 8 + dev[2])
+    bz[z] = by[0] + by[1] + by[2] + by[3]
+    base = 26
+    for dev in zs:
+        go(zin.at[dev[2]], rz.at[z], base + z, dev)
+    for dev in zs:
+        go(bz.at[z], bz.at[z], base + 8 + z, dev)
+    total = zin[z]
+    for dev in zs:
+        land(rz.at[dev[2]], base + dev[2])
+        total = total + rz[dev[2]]
+    zfull[z] = total
+    base = 42
+    for dev in zs:
+        go(zfull.at[z], zfull.at[z], base + z, dev)
+    for dev in zs:
+        land(bz.at[dev[2]], 34 + dev[2])
+    bout[...] = (((bz[0] + bz[1]) + (bz[2] + bz[3])) + ((bz[4] + bz[5]) + (bz[6] + bz[7])))
+    for dev in zs:
+        land(zfull.at[dev[2]], base + dev[2])
+    base = 50
+    for h, (own, line, me) in enumerate(((x, ys, y), (y, xs, x))):
+        rows = pl.ds(pl.multiple_of(h * A + own * B, B), B)
+        lane0 = core * 512
+
+        def at(j):
+            return pl.ds(pl.multiple_of(lane0 + j * 128, 128), 128)
+
+        gout[rows, at(me)] = zfull[h * 4 : h * 4 + 4].reshape(96, 128).astype(BF)
+        for dev in line:
+            go(gout.at[rows, at(me)], gout.at[rows, at(me)], base + h * 4 + me, dev)
+    for h, (own, line, me) in enumerate(((x, ys, y), (y, xs, x))):
+        rows = pl.ds(pl.multiple_of(h * A + own * B, B), B)
+        lane0 = core * 512
+        for dev in line:
+            piece = gout.at[rows, pl.ds(pl.multiple_of(lane0 + dev[2] * 128, 128), 128)]
+            land(piece, base + h * 4 + dev[2])
+    base = 58
+    for h, (line, me) in enumerate(((xs, x), (ys, y))):
+        rows = pl.ds(pl.multiple_of(h * A + me * B, B), B)
+        for dev in line:
+            go(gout.at[rows, mine], gout.at[rows, mine], base + h * 4 + me, dev)
+        go(gout.at[rows, mine], gout.at[rows, mine], 66 + h * 4 + me, sibling[0])
+    for h, (line, me) in enumerate(((xs, x), (ys, y))):
+        for dev in line:
+            rows = pl.ds(pl.multiple_of(h * A + dev[2] * B, B), B)
+            land(gout.at[rows, mine], base + h * 4 + dev[2])
+            go(gout.at[rows, mine], gout.at[rows, mine], 66 + h * 4 + dev[2], sibling[0])
+    for h in range(2):
+        for j in range(4):
+            rows = pl.ds(h * A + j * B, B)
+            land(gout.at[rows, other], 66 + h * 4 + j)
+    for c in sent:
+        c.wait_send()
+
+
+AR_SCRATCH = [
+    pltpu.VMEM((768, 512), BF),
+    pltpu.VMEM((768, 512), BF),
+    pltpu.VMEM((2, 4, 96, 512), BF),
+    pltpu.VMEM((2, 96, 512), BF),
+    pltpu.VMEM((2, 4, 96, 128), BF),
+    pltpu.VMEM((8, 24, 128), F32),
+    pltpu.VMEM((8, 24, 128), F32),
+    pltpu.VMEM((24, 128), F32),
+    pltpu.VMEM((8, 24, 128), F32),
+    pltpu.VMEM((16, 128), F32),
+    pltpu.VMEM((4, 16, 128), F32),
+    pltpu.VMEM((4, 16, 128), F32),
+    pltpu.VMEM((8, 16, 128), F32),
+    pltpu.SemaphoreType.DMA((80,)),
+    pltpu.SemaphoreType.DMA((80,)),
+]
+
+
+def greet(devs):
+    barrier = pltpu.get_barrier_semaphore()
+    for dev in devs:
+        pl.semaphore_signal(barrier, inc=1, device_id=(dev[0], dev[1]), device_id_type=MESH)
+    pl.semaphore_wait(barrier, len(devs))
+
+
+def ar_kernel(g, bias, gout, bout, *scratch):
+    sibling, xs, ys, zs = partners()
+    greet(sibling + xs + ys + zs)
+    reduce_all(g, bias, gout, bout, *scratch)
+
+
+def all_reduce(g, bias):
+    vm = pl.BlockSpec(memory_space=pltpu.VMEM)
+    return pl.pallas_call(
+        ar_kernel,
+        out_shape=(jax.ShapeDtypeStruct((768, 1024), BF), jax.ShapeDtypeStruct((16, 128), F32)),
+        in_specs=[vm, vm], out_specs=(vm, vm), scratch_shapes=AR_SCRATCH,
+        compiler_params=pltpu.CompilerParams(collective_id=0, has_side_effects=True,
+                                             vmem_limit_bytes=32 << 20),
+        name="reduce_grads",
+    )(g, bias)
 
 
 def extended(block, sides, width):
@@ -24,9 +219,13 @@
 
 
 def reduce_grads(partials):
-    return lax.psum(
-        (partials[0], partials[1], partials[2], partials[3], partials[4]), ("row", "col")
-    )
+    g = jnp.concatenate([partials[0], partials[1], partials[3]], axis=0).astype(BF)
+    bias = jnp.concatenate(
+        [partials[2], partials[4], jnp.zeros((768,), F32)]).reshape(16, 128)
+    g, bias = all_reduce(g, bias)
+    g = g.astype(F32)
+    bias = bias.reshape(-1)
+    return g[:256], g[256:512], bias[:1024], g[512:].T, bias[1024:1280]
 
 
 def adjoint_part(adjacency, d_aggregate, local_idx, block_rows, tile_size, per_row, width):
@@ -81,7 +280,7 @@
         jnp.dot(node_features.T, d_hidden, preferred_element_type=jnp.float32),
         jnp.dot(aggregate.T, d_hidden, preferred_element_type=jnp.float32),
         jnp.sum(d_hidden.astype(jnp.float32), axis=0),
-        jnp.dot(hidden.T, cotangent, preferred_element_type=jnp.float32),
+        jnp.dot(cotangent.T, hidden, preferred_element_type=jnp.float32),
         jnp.sum(cotangent.astype(jnp.float32), axis=0),
     )
     d_aggregate = jnp.dot(d_hidden, w_neigh.T, preferred_element_type=jnp.float32).astype(

time: 390 us -> 178 us (0.46)
  waiting for transfers between devices: 184 us -> 15.6 us
  blocking collectives: 100 us -> 0 us
  Pallas kernels: 0 us -> 69.2 us
  between operations: 14.2 us -> 0.87 us
    psum x1 -> x0, waiting for transfers between devices: 168 us -> none  [reduce_grads(): lax.psum((partials[0], partials[1], partials[2], partials[3], partials[4]...]
    psum x1 -> x0, blocking collectives: 100 us -> none  [reduce_grads(): lax.psum((partials[0], partials[1], partials[2], partials[3], partials[4]...]
    pallas_call x0 -> x1, Pallas kernels: none -> 69.2 us  [all_reduce(): pl.pallas_call(ar_kernel, out_shape=(jax.ShapeDtypeStruct((768, 1024), BF...]
    ppermute x2, waiting for transfers between devices: 12.7 us -> 4.53 us  [extended(): lax.ppermute(lax.slice_in_dim(block, block.shape[dim] - width, None, axis...]
    ppermute x2, waiting for transfers between devices: 3.51 us -> 11.1 us  [extended(): lax.ppermute(lax.slice_in_dim(block, 0, width, axis=dim), axis, backward)]
  transfers between devices with their start and end apart: 5 -> 4, of which waited for: 3 -> 2; matrix products, arithmetic and copies ran while one was open for 4% -> 9% of each run, Pallas kernels for 0% -> 39%
where the time goes in v1:
time: 178 us
  Pallas kernels  69.2 us (39%)
  other arithmetic  32.9 us (18%)
  matrix products  29.7 us (17%)
  starting transfers between devices  17.4 us (10%)
  waiting for transfers between devices  15.6 us (9%)
  local copies, waits for them, and re-layouts  11.9 us (7%)
    pallas_call x1, Pallas kernels, all_reduce(): pl.pallas_call(ar_kernel, out_shape=(jax.ShapeDtypeStruct((768, 1024), BF...  69.2 us
    scatter-add x1, other arithmetic, adjoint_part(): spread_sum = spread_sum.at[local_idx.reshape(-1)].add(spread)  26.5 us
    ppermute x2, waiting for transfers between devices, extended(): lax.ppermute(lax.slice_in_dim(block, 0, width, axis=dim), axis, backward)  11.1 us
    ppermute x2, starting transfers between devices, extended(): lax.ppermute(lax.slice_in_dim(block, 0, width, axis=dim), axis, backward)  10.5 us
    ppermute x2, starting transfers between devices, extended(): lax.ppermute(lax.slice_in_dim(block, block.shape[dim] - width, None, axis...  6.85 us
    ppermute x2, waiting for transfers between devices, extended(): lax.ppermute(lax.slice_in_dim(block, block.shape[dim] - width, None, axis...  4.53 us
    dot_general x1, matrix products, adjoint_part(): jnp.einsum('bij,bif->bjf', adjacency, d_aggregate.reshape(block_rows, til...  4.52 us
    dot_general x1, matrix products, local(): jnp.dot(node_features, w_self, preferred_element_type=jnp.float32)  3.92 us
  transfers between devices with their start and end apart: 4, of which 2 were waited for; matrix products, arithmetic and copies ran while one was open for 9% of the time, Pallas kernels for 39%

profile of v1, /device:TPU:1, one launch (start us, length us, event | category | flops | bytes accessed | tf_op | source)
XLA Modules:
  0.0 177.5 jit_solution(10331042699743250589)
XLA Ops:
  0.6 0.0 copy-start
  0.6 4.5 %collective-permute-start = (bf16[1024,256]{1,0:T(8,128)(2,1)}, bf16[1024,256]{1,0:T(8,128)(2,1)S(1)}, u32[]{:S(2)}, u32[]{:S(2)}) collective-permute-start(bf16[1024,256]{1,0:T(8,128)(2,1)} %param.9), channel_id=1, source_target_pairs={{0,1},{1,2},{2,3},{3,4},{4,5},{5,6},{6,7},{7,8},{8,9},{9,10},{10,1... | collective-permute-start | bytes 1572872 | tf_op jit(solution)/shard_map/ppermute | solution.py:209
  5.2 5.2 %collective-permute-start.1 = (bf16[1024,256]{1,0:T(8,128)(2,1)}, bf16[1024,256]{1,0:T(8,128)(2,1)}, u32[]{:S(2)}, u32[]{:S(2)}) collective-permute-start(bf16[1024,256]{1,0:T(8,128)(2,1)} %param.9), channel_id=1, source_target_pairs={{1,0},{2,1},{3,2},{4,3},{5,4},{6,5},{7,6},{8,7},{9,8},{10,9},{11,1... | collective-permute-start | bytes 1572872 | tf_op jit(solution)/shard_map/ppermute | solution.py:212
  10.4 0.7 compare_select_fusion
  11.1 0.1 copy.19
  11.1 0.1 reshape.83
  11.2 0.1 copy.20
  11.3 0.1 reshape.77
  11.4 1.2 convert_reduce_fusion.1
  12.6 0.0 copy-start.4
  12.6 3.9 %fusion.19 = f32[1024,1024]{1,0:T(8,128)} fusion(bf16[1024,256]{1,0:T(8,128)(2,1)} %param.9, bf16[256,1024]{1,0:T(8,128)(2,1)} %param.12), kind=kOutput, calls=%fused_computation.47 | convolution fusion | flops 536870912 | bytes 5242880 | tf_op jit(solution)/shard_map/dot_general | solution.py:268
  16.5 4.5 %collective-permute-done = bf16[1024,256]{1,0:T(8,128)(2,1)S(1)} collective-permute-done((bf16[1024,256]{1,0:T(8,128)(2,1)}, bf16[1024,256]{1,0:T(8,128)(2,1)S(1)}, u32[]{:S(2)}, u32[]{:S(2)}) %collective-permute-start) | collective-permute-done | bytes 524320 | tf_op jit(solution)/shard_map/ppermute | solution.py:209
  21.1 11.1 %collective-permute-done.1 = bf16[1024,256]{1,0:T(8,128)(2,1)} collective-permute-done((bf16[1024,256]{1,0:T(8,128)(2,1)}, bf16[1024,256]{1,0:T(8,128)(2,1)}, u32[]{:S(2)}, u32[]{:S(2)}) %collective-permute-start.1) | collective-permute-done | bytes 524320 | tf_op jit(solution)/shard_map/ppermute | solution.py:212
  32.2 0.0 copy-done.4
  32.2 1.1 pad_maximum_fusion
  33.3 2.8 %gather_fusion = bf16[128,64,256]{2,1,0:T(8,128)(2,1)} fusion(bf16[48,64,256]{2,1,0:T(8,128)(2,1)S(1)} %bitcast.50, s32[1024]{0:T(1024)S(1)} %pad_clamp_fusion), kind=kCustom, calls=%fused_computation | custom fusion | bytes 8389120 | tf_op jit(solution)/shard_map/gather | solution.py:263
  36.1 3.7 %convolution_convert_fusion = bf16[16,64,256]{2,1,0:T(8,128)(2,1)S(1)} fusion(bf16[16,512,256]{2,1,0:T(8,128)(2,1)} %bitcast.51, s32[16,64,512]{2,1,0:T(8,128)} %param.11), kind=kOutput, calls=%fused_computation.18 | convolution fusion | flops 270270464 | bytes 6815744 | tf_op jit(solution)/shard_map/bij,bjf->bif/dot_general | solution.py:265
  39.9 0.0 copy-done
  39.9 0.3 copy-done.1
  40.1 0.0 copy-done.11
  40.2 3.3 %multiply_convert_fusion = (bf16[1024,1024]{1,0:T(8,128)(2,1)}, f32[1024,1024]{1,0:T(8,128)S(1)}) fusion(f32[1024]{0:T(1024)S(1)} %copy-done.11, f32[1024,1024]{1,0:T(8,128)S(1)} %copy-done.1, bf16[1024,256]{1,0:T(8,128)(2,1)S(1)} %bitcast.52, bf16[256,1024]{1,0:T(8,128)(2,1)S(1)} %copy-done), kind=kOutput, calls=%fused_computation.12 | convolution fusion | flops 548405248 | bytes 11538432 | tf_op jit(solution)/shard_map/dot_general | solution.py:269
  43.4 0.0 copy-done.7
  43.4 0.0 copy-done.10
  43.4 3.3 %convert_reduce_fusion = (f32[1024]{0:T(1024)S(1)}, bf16[1024,1024]{1,0:T(8,128)(2,1)S(1)}) fusion(f32[1024,1024]{1,0:T(8,128)S(1)} %get-tuple-element.34, bf16[1024,256]{1,0:T(8,128)(2,1)S(1)} %copy-done.7, bf16[1024,256]{1,0:T(8,128)(2,1)S(1)} %copy-done.10), kind=kOutput, calls=%fused_computation.11 | convolution fusion | flops 559938560 | bytes 7344128 | tf_op jit(solution)/shard_map/dot_general | solution.py:277
  46.8 0.7 convolution_convert_fusion.4
  47.5 0.0 copy-start.2
  47.5 1.5 convolution_convert_fusion.2
  49.1 1.6 fusion.8
  50.6 0.0 copy-done.2
  50.6 4.5 %fusion.14 = f32[16,512,256]{2,1,0:T(8,128)} fusion(bf16[16,64,256]{2,1,0:T(8,128)(2,1)S(1)} %bitcast.54, s32[16,64,512]{2,1,0:T(8,128)S(1)} %copy-done.2), kind=kOutput, calls=%fused_computation.35 | convolution fusion | flops 270008320 | bytes 11010048 | tf_op jit(solution)/shard_map/bij,bif->bjf/dot_general | solution.py:233
  55.2 2.1 %broadcast_in_dim.13 = f32[48,64,256]{2,1,0:T(8,128)} broadcast(f32[]{:T(128)} %constant.15.clone.1), dimensions={} | broadcast | bytes 3145732 | tf_op jit(solution)/shard_map/broadcast_in_dim | solution.py:240
  57.2 26.5 %scatter_fusion = f32[48,64,256]{2,1,0:T(8,128)} fusion(f32[48,64,256]{2,1,0:T(8,128)} %broadcast_in_dim.13, s32[128]{0:T(128)S(1)} %fusion.15, f32[128,64,256]{2,1,0:T(8,128)} %bitcast.49), kind=kCustom, calls=%fused_computation.1 | custom fusion | flops 2097152 | bytes 25166336 | tf_op jit(solution)/shard_map/scatter-add | solution.py:241
  83.7 3.8 %fusion.18 = (f32[16,64,256]{2,1,0:T(8,128)}, f32[16,64,256]{2,1,0:T(8,128)}, f32[16,64,256]{2,1,0:T(8,128)}) fusion(f32[48,64,256]{2,1,0:T(8,128)} %scatter_fusion), kind=kLoop, calls=%fused_computation.46 | loop fusion | bytes 6291456 | tf_op jit(solution)/shard_map/slice | solution.py:245
  87.5 2.3 %collective-permute-start.2 = (f32[1024,256]{1,0:T(8,128)}, f32[1024,256]{1,0:T(8,128)}, u32[]{:S(2)}, u32[]{:S(2)}) collective-permute-start(f32[1024,256]{1,0:T(8,128)} %bitcast.7), channel_id=1, source_target_pairs={{0,1},{1,2},{2,3},{3,4},{4,5},{5,6},{6,7},{7,8},{8,9},{9,10},{10,1... | collective-permute-start | bytes 3145736 | tf_op jit(solution)/shard_map/ppermute | solution.py:209
  89.9 5.3 %collective-permute-start.3 = (f32[1024,256]{1,0:T(8,128)}, f32[1024,256]{1,0:T(8,128)}, u32[]{:S(2)}, u32[]{:S(2)}) collective-permute-start(f32[1024,256]{1,0:T(8,128)} %bitcast.8), channel_id=1, source_target_pairs={{1,0},{2,1},{3,2},{4,3},{5,4},{6,5},{7,6},{8,7},{9,8},{10,9},{11,1... | collective-permute-start | bytes 3145736 | tf_op jit(solution)/shard_map/ppermute | solution.py:212
  95.2 0.8 fusion.9
  96.0 0.1 pad_maximum_fusion.1.g
  96.1 69.2 %reduce_grads.1 = (bf16[768,1024]{1,0:T(8,128)(2,1)S(1)}, f32[16,128]{1,0:T(8,128)S(1)}) custom-call(bf16[768,1024]{1,0:T(8,128)(2,1)S(1)} %pad_maximum_fusion.1.g, f32[16,128]{1,0:T(8,128)S(1)} %maximum_bitcast_fusion.bias), custom_call_target="tpu_custom_call" | custom-call | tf_op jit(solution)/shard_map/reduce_grads/pallas_call | solution.py:194
  165.3 0.4 convert_element_type.48
  165.7 0.0 copy-start.12
  165.7 1.7 fusion.10
  167.5 2.6 %copy.21 = f32[1024,256]{1,0:T(8,128)} copy(f32[1024,256]{0,1:T(8,128)} %get-tuple-element.27) | data formatting | bytes 2097152
  170.1 0.6 multiply_bitcast_fusion.1
  170.6 0.6 multiply_bitcast_fusion
  171.2 3.2 %fusion.7 = bf16[1024,256]{1,0:T(8,128)(2,1)} fusion(bf16[1024,1024]{1,0:T(8,128)(2,1)} %get-tuple-element.33, bf16[1024,256]{1,0:T(8,128)(2,1)} %param.15, f32[256]{0:T(256)S(1)} %copy-done.12), kind=kOutput, calls=%fused_computation.23 | convolution fusion | flops 537395200 | bytes 3146752 | tf_op jit(solution)/shard_map/dot_general | solution.py:274
  174.4 0.0 collective-permute-done.2
  174.4 0.0 collective-permute-done.3
  174.4 3.1 %fusion.13 = bf16[1024,256]{1,0:T(8,128)(2,1)} fusion(f32[1024,256]{1,0:T(8,128)} %collective-permute-done.3, f32[1024,256]{1,0:T(8,128)} %collective-permute-done.2, f32[16,64,256]{2,1,0:T(8,128)S(1)} %copy-done.3, bf16[1024,1024]{1,0:T(8,128)(2,1)S(1)} %get-tuple-element.36, bf16[256,1024]{1,0:T(8,128)(2,1)S(1)} %copy-done.5), kind=kOutput, calls=%fused_computation.33 | convolution fusion | flops 537919488 | bytes 6291456 | tf_op jit(solution)/shard_map/dot_general | solution.py:289
  (21 shorter events, 0.1 us)
Async XLA Ops:
  0.6 39.2 %copy-start = (bf16[256,1024]{1,0:T(8,128)(2,1)S(1)}, bf16[256,1024]{1,0:T(8,128)(2,1)}, u32[]{:S(2)}) copy-start(bf16[256,1024]{1,0:T(8,128)(2,1)} %param.13) | copy-start | bytes 1572868
  0.6 20.4 %collective-permute-start = (bf16[1024,256]{1,0:T(8,128)(2,1)}, bf16[1024,256]{1,0:T(8,128)(2,1)S(1)}, u32[]{:S(2)}, u32[]{:S(2)}) collective-permute-start(bf16[1024,256]{1,0:T(8,128)(2,1)} %param.9), channel_id=1, source_target_pairs={{0,1},{1,2},{2,3},{3,4},{4,5},{5,6},{6,7},{7,8},{8,9},{9,10},{10,1... | collective-permute-start | bytes 1572872 | tf_op jit(solution)/shard_map/ppermute | solution.py:209
  5.2 27.0 %collective-permute-start.1 = (bf16[1024,256]{1,0:T(8,128)(2,1)}, bf16[1024,256]{1,0:T(8,128)(2,1)}, u32[]{:S(2)}, u32[]{:S(2)}) collective-permute-start(bf16[1024,256]{1,0:T(8,128)(2,1)} %param.9), channel_id=1, source_target_pairs={{1,0},{2,1},{3,2},{4,3},{5,4},{6,5},{7,6},{8,7},{9,8},{10,9},{11,1... | collective-permute-start | bytes 1572872 | tf_op jit(solution)/shard_map/ppermute | solution.py:212
  12.6 19.6 %copy-start.4 = (bf16[1024,256]{1,0:T(8,128)(2,1)S(1)}, bf16[1024,256]{1,0:T(8,128)(2,1)}, u32[]{:S(2)}) copy-start(bf16[1024,256]{1,0:T(8,128)(2,1)} %param.9) | copy-start | bytes 1572868
  36.1 4.0 %copy-start.1 = (f32[1024,1024]{1,0:T(8,128)S(1)}, f32[1024,1024]{1,0:T(8,128)}, u32[]{:S(2)}) copy-start(f32[1024,1024]{1,0:T(8,128)} %fusion.19) | copy-start | bytes 12582916
  36.1 4.0 %copy-start.11 = (f32[1024]{0:T(1024)S(1)}, f32[1024]{0:T(1024)}, u32[]{:S(2)}) copy-start(f32[1024]{0:T(1024)} %param.14) | copy-start | bytes 12292
  40.1 3.3 %copy-start.7 = (bf16[1024,256]{1,0:T(8,128)(2,1)S(1)}, bf16[1024,256]{1,0:T(8,128)(2,1)}, u32[]{:S(2)}) copy-start(bf16[1024,256]{1,0:T(8,128)(2,1)} %param.17) | copy-start | bytes 1572868
  40.2 3.3 %copy-start.10 = (bf16[1024,256]{1,0:T(8,128)(2,1)S(1)}, bf16[1024,256]{1,0:T(8,128)(2,1)}, u32[]{:S(2)}) copy-start(bf16[1024,256]{1,0:T(8,128)(2,1)} %param.15) | copy-start | bytes 1572868
  47.5 3.1 %copy-start.2 = (s32[16,64,512]{2,1,0:T(8,128)S(1)}, s32[16,64,512]{2,1,0:T(8,128)}, u32[]{:S(2)}) copy-start(s32[16,64,512]{2,1,0:T(8,128)} %param.11) | copy-start | bytes 6291460
  83.7 11.5 %copy-start.8 = (bf16[1024,256]{1,0:T(8,128)(2,1)S(1)}, bf16[1024,256]{1,0:T(8,128)(2,1)}, u32[]{:S(2)}) copy-start(bf16[1024,256]{1,0:T(8,128)(2,1)} %param.17) | copy-start | bytes 1572868
  83.7 11.5 %copy-start.13 = (bf16[1024,1024]{1,0:T(8,128)(2,1)S(1)}, bf16[1024,1024]{1,0:T(8,128)(2,1)}, u32[]{:S(2)}) copy-start(bf16[1024,1024]{1,0:T(8,128)(2,1)} %get-tuple-element.33) | copy-start | bytes 6291460
  87.5 8.5 %copy-start.6 = (bf16[256,1024]{1,0:T(8,128)(2,1)S(1)}, bf16[256,1024]{1,0:T(8,128)(2,1)}, u32[]{:S(2)}) copy-start(bf16[256,1024]{1,0:T(8,128)(2,1)} %convolution_convert_fusion.2) | copy-start | bytes 1572868
  87.5 8.5 %copy-start.9 = (bf16[256,1024]{1,0:T(8,128)(2,1)S(1)}, bf16[256,1024]{1,0:T(8,128)(2,1)}, u32[]{:S(2)}) copy-start(bf16[256,1024]{1,0:T(8,128)(2,1)} %fusion.8) | copy-start | bytes 1572868
  87.5 86.9 %collective-permute-start.2 = (f32[1024,256]{1,0:T(8,128)}, f32[1024,256]{1,0:T(8,128)}, u32[]{:S(2)}, u32[]{:S(2)}) collective-permute-start(f32[1024,256]{1,0:T(8,128)} %bitcast.7), channel_id=1, source_target_pairs={{0,1},{1,2},{2,3},{3,4},{4,5},{5,6},{6,7},{7,8},{8,9},{9,10},{10,1... | collective-permute-start | bytes 3145736 | tf_op jit(solution)/shard_map/ppermute | solution.py:209
  89.9 84.5 %collective-permute-start.3 = (f32[1024,256]{1,0:T(8,128)}, f32[1024,256]{1,0:T(8,128)}, u32[]{:S(2)}, u32[]{:S(2)}) collective-permute-start(f32[1024,256]{1,0:T(8,128)} %bitcast.8), channel_id=1, source_target_pairs={{1,0},{2,1},{3,2},{4,3},{5,4},{6,5},{7,6},{8,7},{9,8},{10,9},{11,1... | collective-permute-start | bytes 3145736 | tf_op jit(solution)/shard_map/ppermute | solution.py:212
  165.7 5.5 %copy-start.12 = (f32[256]{0:T(256)S(1)}, f32[256]{0:T(256)}, u32[]{:S(2)}) copy-start(f32[256]{0:T(256)} %param.16) | copy-start | bytes 3076
  167.5 6.9 %copy-start.5 = (bf16[256,1024]{1,0:T(8,128)(2,1)S(1)}, bf16[256,1024]{1,0:T(8,128)(2,1)}, u32[]{:S(2)}) copy-start(bf16[256,1024]{1,0:T(8,128)(2,1)} %param.12) | copy-start | bytes 1572868
  170.1 4.4 %copy-start.3 = (f32[16,64,256]{2,1,0:T(8,128)S(1)}, f32[16,64,256]{2,1,0:T(8,128)}, u32[]{:S(2)}) copy-start(f32[16,64,256]{2,1,0:T(8,128)} %get-tuple-element.30) | copy-start | bytes 3145732

commit v2 on v1

--- a/solution.py
+++ b/solution.py
@@ -1,5 +1,7 @@
-import functools, math
-import jax, jax.numpy as jnp
+import math
+
+import jax
+import jax.numpy as jnp
 from jax import lax
 from jax.experimental import pallas as pl
 from jax.experimental.pallas import tpu as pltpu
@@ -37,7 +39,7 @@
 
 
 def reduce_all(g, bias, gout, bout, rc, s1, r1, t1, r2, zin, rz, zc, zfull, bc, bx, by, bz,
-               send, recv):
+               send, recv, hook=None):
     row, z_lo, core, x, y, z = coords()
     sibling, xs, ys, zs = partners()
     A, B = 384, 96
@@ -57,6 +59,8 @@
     other = pl.ds(pl.multiple_of((1 - core) * 512, 512), 512)
     go(g.at[:, other], rc, 0, sibling[0])
     go(bias, bc, 1, sibling[0])
+    if hook is not None:
+        hook()
     land(rc, 0)
     land(bc, 1)
 
@@ -183,123 +187,296 @@
     pl.semaphore_wait(barrier, len(devs))
 
 
-def ar_kernel(g, bias, gout, bout, *scratch):
+SCALE_TILE = 0.25 / math.sqrt(512)
+C0 = math.sqrt(2.0 / math.pi)
+C1 = C0 * 0.044715
+T_RHS = (((1,), (1,)), ((), ()))
+
+
+def mm(a, b):
+    return jnp.dot(a, b, preferred_element_type=F32)
+
+
+def mm_t(a, b):
+    return lax.dot_general(a, b, T_RHS, preferred_element_type=F32)
+
+
+def ds256(i):
+    return pl.ds(pl.multiple_of(i * 256, 256), 256)
+
+
+def neighbours():
+    row, z_lo, core, x, y, z = coords()
+    here = row * 4 + z_lo
+    right = (here + 1) % 256
+    left = (here + 255) % 256
+    return here, (left // 4, left % 4), (right // 4, right % 4)
+
+
+def layer_kernel(
+    cols, x_hbm, tw_hbm, ws_hbm, wn_hbm, bh, wo_hbm, bo, cot_hbm,
+    embed, gradf, gout, bout,
+    win, tw, ws, wn, wo, cot, dup, dense, dense_t, pre, dact, agg0, agg, xt, ct, at,
+    hid, dh, dagg, bsum, own, lo, hi, lo_b, hi_b, from_r, from_l, g, bias,
+    in_sem, halo_send, halo_recv, *ar,
+):
+    here, left, right = neighbours()
     sibling, xs, ys, zs = partners()
-    greet(sibling + xs + ys + zs)
-    reduce_all(g, bias, gout, bout, *scratch)
-
-
-def all_reduce(g, bias):
-    vm = pl.BlockSpec(memory_space=pltpu.VMEM)
-    return pl.pallas_call(
-        ar_kernel,
-        out_shape=(jax.ShapeDtypeStruct((768, 1024), BF), jax.ShapeDtypeStruct((16, 128), F32)),
-        in_specs=[vm, vm], out_specs=(vm, vm), scratch_shapes=AR_SCRATCH,
-        compiler_params=pltpu.CompilerParams(collective_id=0, has_side_effects=True,
-                                             vmem_limit_bytes=32 << 20),
-        name="reduce_grads",
-    )(g, bias)
-
-
-def extended(block, sides, width):
-    for axis, dim in sides:
-        count = lax.axis_size(axis)
-        forward = [(i, i + 1) for i in range(count - 1)]
-        backward = [(target, source) for source, target in forward]
-        low = lax.ppermute(
-            lax.slice_in_dim(block, block.shape[dim] - width, None, axis=dim), axis, forward
-        )
-        high = lax.ppermute(lax.slice_in_dim(block, 0, width, axis=dim), axis, backward)
-        block = jnp.concatenate([low, block, high], axis=dim)
-    return block
-
-
-def gelu_tanh(values):
-    return jax.nn.gelu(values, approximate=True)
-
-
-def reduce_grads(partials):
-    g = jnp.concatenate([partials[0], partials[1], partials[3]], axis=0).astype(BF)
-    bias = jnp.concatenate(
-        [partials[2], partials[4], jnp.zeros((768,), F32)]).reshape(16, 128)
-    g, bias = all_reduce(g, bias)
-    g = g.astype(F32)
-    bias = bias.reshape(-1)
-    return g[:256], g[256:512], bias[:1024], g[512:].T, bias[1024:1280]
-
-
-def adjoint_part(adjacency, d_aggregate, local_idx, block_rows, tile_size, per_row, width):
-    rows_here = block_rows * tile_size
-    spread = jnp.einsum(
-        "bij,bif->bjf",
-        adjacency,
-        d_aggregate.reshape(block_rows, tile_size, width),
-        preferred_element_type=jnp.float32,
-    )
-    spread = spread.reshape(block_rows * per_row, tile_size, width)
-    spread_sum = jnp.zeros((3 * block_rows, tile_size, width), jnp.float32)
-    spread_sum = spread_sum.at[local_idx.reshape(-1)].add(spread)
-    spread_sum = spread_sum.reshape(3 * rows_here, width)
-    outer_parts = jnp.concatenate([spread_sum[:rows_here], spread_sum[2 * rows_here :]], axis=0)
-    padded = extended(outer_parts, ((("row", "col"), 0),), rows_here)
-    return spread_sum[rows_here : 2 * rows_here] + padded[:rows_here] + padded[3 * rows_here :]
+
+    loads = []
+    for n, (src, dst) in enumerate((
+        (tw_hbm, tw), (x_hbm, win.at[pl.ds(1024, 1024), :]), (cot_hbm, cot),
+        (ws_hbm, ws), (wo_hbm, wo), (wn_hbm, wn),
+    )):
+        c = pltpu.make_async_copy(src, dst, in_sem.at[n])
+        c.start()
+        loads.append(c)
+    greet([left, right] + sibling + xs + ys + zs)
+
+    halo = []
+
+    def halo_copy(src, dst, n, dev):
+        c = remote(src, dst, halo_send.at[n], halo_recv.at[n], dev)
+        c.start()
+        halo.append(c)
+
+    for i in range(4):
+        far = pl.ds(256 * (3 - i), 256)
+        near = pl.ds(256 * i, 256)
+        halo_copy(x_hbm.at[far, :], win.at[far, :], 3 - i, right)
+        halo_copy(x_hbm.at[near, :], win.at[pl.ds(2048 + 256 * i, 256), :], 4 + i, left)
+
+    def halo_wait(n):
+        dst = win.at[pl.ds(256 * n if n < 4 else 1024 + 256 * n, 256), :]
+        remote(dst, dst, halo_send.at[n], halo_recv.at[n], left).wait_recv()
+
+    loads[0].wait()
+    lane = lax.broadcasted_iota(jnp.int32, (64, 128), 1)
+    half = lax.broadcasted_iota(jnp.int32, (1, 128), 1) // 64
+
+    @pl.loop(0, 16)
+    def _(p):
+        c = p // 4
+        rows = pl.ds(pl.multiple_of((p % 4) * 64, 64), 64)
+        base = here * 16 - 16 + 4 * c
+        for q in range(4):
+            u = tw[p, :, 128 * q : 128 * q + 128].astype(F32) * SCALE_TILE
+            u = u.astype(BF).astype(F32)
+            r = pltpu.roll(u, 64, 1)
+            dup[2 * q] = jnp.where(lane < 64, u, r)
+            dup[2 * q + 1] = jnp.where(lane < 64, r, u)
+        spot = [cols[p, s] - base for s in range(8)]
+
+        @pl.loop(0, 18)
+        def _(j):
+            total = jnp.zeros((64, 128), F32)
+            for s in range(8):
+                hit = jnp.where(half == spot[s] - 2 * j, 1.0, 0.0).astype(F32)
+                total = total + dup[s] * hit
+            dense[c, rows, pl.ds(pl.multiple_of(j * 128, 128), 128)] = total.astype(BF)
+
+    @pl.loop(0, 36)
+    def _(i):
+        c, t = i // 9, i % 9
+        dense_t[c, ds256(t), :] = dense[c, :, ds256(t)].T
+
+    for c in loads[1:]:
+        c.wait()
+
+    bsum[...] = jnp.zeros_like(bsum)
+
+    @pl.loop(0, 4)
+    def _(c):
+        rows = ds256(c)
+        mine = pl.ds(pl.multiple_of(1024 + c * 256, 256), 256)
+        xc = win[mine, :]
+        cc = cot[rows, :]
+        xt[:, rows] = xc.T
+        ct[:, rows] = cc.T
+        bsum[:, 1024:1280] += jnp.sum(cc.astype(F32).reshape(32, 8, 256), axis=0)
+        for n in range(4):
+            n4 = slice(256 * n, 256 * n + 256)
+            pre[rows, n4] = mm(xc, ws[:, n4]) + bh[:, n4]
+            dact[rows, n4] = mm_t(cc, wo[n4, :])
+        total = jnp.zeros((256, 256), F32)
+        for t in range(4):
+            total = total + mm(dense[c, :, ds256(4 + t - c)], win[1024 + 256 * t : 1280 + 256 * t, :])
+        agg0[rows, :] = total
+
+    lo[...] = jnp.zeros_like(lo)
+    hi[...] = jnp.zeros_like(hi)
+
+    def adjoint_send(n, buf, src, dst, dev):
+        piece = pl.ds(256 * (n % 4), 256)
+        buf[piece, :] = src[piece, :].astype(BF)
+        halo_copy(buf.at[piece, :], dst.at[piece, :], 8 + n, dev)
+
+    @pl.loop(0, 4)
+    def _(k):
+        c = (k + 1) % 3 + 2 * (k // 3)
+
+        @pl.when(k == 0)
+        def _():
+            for n in (3, 4, 2, 5, 1):
+                halo_wait(n)
+
+        @pl.when(k == 1)
+        def _():
+            halo_wait(6)
+
+        @pl.when(k == 2)
+        def _():
+            halo_wait(0)
+
+        @pl.when(k == 3)
+        def _():
+            halo_wait(7)
+
+        rows = ds256(c)
+        total = agg0[rows, :]
+        for t in range(5):
+            w = c + t + 4 * ((c + t) // 4)
+            total = total + mm(dense[c, :, ds256(w - c)], win[ds256(w), :])
+        ag = total.astype(BF)
+        agg[rows, :] = ag
+        for n in range(4):
+            n4 = slice(256 * n, 256 * n + 256)
+            pre[rows, n4] += mm(ag, wn[:, n4])
+
+        @pl.loop(0, 8)
+        def _(i):
+            r = pl.ds(pl.multiple_of(c * 256 + i * 32, 32), 32)
+            for n in range(4):
+                n4 = slice(256 * n, 256 * n + 256)
+                v = pre[r, n4]
+                u = v * v
+                th = jnp.tanh(v * (C0 + C1 * u))
+                a = 0.5 * th + 0.5
+                hid[r, n4] = (v * a).astype(BF)
+                slope = a + (0.5 * v) * (1.0 - th * th) * (C0 + (3.0 * C1) * u)
+                d = (dact[r, n4] * slope).astype(BF)
+                dh[r, n4] = d
+                bsum[:, n4] += jnp.sum(d.astype(F32).reshape(4, 8, 256), axis=0)
+
+        da = mm_t(dh[rows, :], wn[...]).astype(BF)
+        dagg[rows, :] = da
+        for t in range(4):
+            @pl.when(c + t < 4)
+            def _():
+                lo[ds256(c + t), :] += mm(dense_t[c, ds256(t), :], da)
+
+            @pl.when(t <= c)
+            def _():
+                hi[pl.ds(256 * t, 256), :] += mm(dense_t[c, ds256(8 - c + t), :], da)
+
+    for n in (3, 2, 1, 0):
+        adjoint_send(4 + n, hi_b, hi, from_l, right)
+        adjoint_send(3 - n, lo_b, lo, from_r, left)
+
+    for c in range(4):
+        at[:, 256 * c : 256 * c + 256] = agg[256 * c : 256 * c + 256, :].T
+    for n in range(4):
+        n4 = slice(256 * n, 256 * n + 256)
+        g[0:256, n4] = mm(xt[...], dh[:, n4]).astype(BF)
+        g[256:512, n4] = mm(at[...], dh[:, n4]).astype(BF)
+        g[512:768, n4] = mm(ct[...], hid[:, n4]).astype(BF)
+    sums = jnp.sum(bsum[...], axis=0, keepdims=True)
+    for n in range(10):
+        bias[n : n + 1, :] = sums[:, 128 * n : 128 * n + 128]
+    bias[10:16, :] = jnp.zeros((6, 128), F32)
+
+    def local_rest():
+        @pl.loop(0, 4)
+        def _(c):
+            rows = ds256(c)
+            embed[rows, :] = (mm(hid[rows, :], wo[...]) + bo[...]).astype(BF)
+            total = mm_t(dh[rows, :], ws[...])
+            for b in range(4):
+                total = total + mm(dense_t[b, ds256(4 + c - b), :], dagg[256 * b : 256 * b + 256, :])
+            own[rows, :] = total
+
+    reduce_all(g, bias, gout, bout, *ar, hook=local_rest)
+
+    for n in (3, 2, 1, 0):
+        for m, dst in ((4 + n, from_l), (3 - n, from_r)):
+            piece = dst.at[pl.ds(256 * (m % 4), 256), :]
+            remote(piece, piece, halo_send.at[8 + m], halo_recv.at[8 + m], left).wait_recv()
+
+    @pl.loop(0, 16)
+    def _(i):
+        r = pl.ds(pl.multiple_of(i * 64, 64), 64)
+        gradf[r, :] = (own[r, :] + from_l[r, :].astype(F32) + from_r[r, :].astype(F32)).astype(BF)
+
+    for c in halo:
+        c.wait_send()
+
+
+LAYER_SCRATCH = [
+    pltpu.VMEM((3072, 256), BF),
+    pltpu.VMEM((16, 64, 512), jnp.int32),
+    pltpu.VMEM((256, 1024), BF),
+    pltpu.VMEM((256, 1024), BF),
+    pltpu.VMEM((1024, 256), BF),
+    pltpu.VMEM((1024, 256), BF),
+    pltpu.VMEM((8, 64, 128), F32),
+    pltpu.VMEM((4, 256, 2304), BF),
+    pltpu.VMEM((4, 2304, 256), BF),
+    pltpu.VMEM((1024, 1024), F32),
+    pltpu.VMEM((1024, 1024), F32),
+    pltpu.VMEM((1024, 256), F32),
+    pltpu.VMEM((1024, 256), BF),
+    pltpu.VMEM((256, 1024), BF),
+    pltpu.VMEM((256, 1024), BF),
+    pltpu.VMEM((256, 1024), BF),
+    pltpu.VMEM((1024, 1024), BF),
+    pltpu.VMEM((1024, 1024), BF),
+    pltpu.VMEM((1024, 256), BF),
+    pltpu.VMEM((8, 1280), F32),
+    pltpu.VMEM((1024, 256), F32),
+    pltpu.VMEM((1024, 256), F32),
+    pltpu.VMEM((1024, 256), F32),
+    pltpu.VMEM((1024, 256), BF),
+    pltpu.VMEM((1024, 256), BF),
+    pltpu.VMEM((1024, 256), BF),
+    pltpu.VMEM((1024, 256), BF),
+    pltpu.VMEM((768, 1024), BF),
+    pltpu.VMEM((16, 128), F32),
+    pltpu.SemaphoreType.DMA((6,)),
+    pltpu.SemaphoreType.DMA((16,)),
+    pltpu.SemaphoreType.DMA((16,)),
+]
 
 
 def local(
     node_features, tile_cols, tile_weights, w_self, w_neigh, bias_hidden, w_out, bias_out, cotangent
 ):
-    rows_here = node_features.shape[0]
-    width = node_features.shape[1]
-    tile_size = tile_weights.shape[1]
-    per_row = tile_cols.shape[1]
-    block_rows = rows_here // tile_size
-    devices_all = lax.axis_size(("row", "col"))
-    tile_scale = 0.25 / math.sqrt(per_row * tile_size)
-    grad_scale = 1.0 / math.sqrt(rows_here * devices_all)
-    window = extended(node_features, ((("row", "col"), 0),), rows_here)
-    first_block = lax.axis_index(("row", "col")) * block_rows - block_rows
-    local_idx = tile_cols - first_block
-    all_blocks = window.reshape(3 * block_rows, tile_size, width)
-    gathered = all_blocks[local_idx].reshape(block_rows, per_row * tile_size, width)
-    adjacency = (tile_weights.astype(jnp.float32) * tile_scale).astype(jnp.bfloat16)
-    aggregate = jnp.einsum("bij,bjf->bif", adjacency, gathered, preferred_element_type=jnp.float32)
-    aggregate = aggregate.reshape(rows_here, width).astype(jnp.bfloat16)
-    preact = (
-        jnp.dot(node_features, w_self, preferred_element_type=jnp.float32)
-        + jnp.dot(aggregate, w_neigh, preferred_element_type=jnp.float32)
-        + bias_hidden
+    vm = pl.BlockSpec(memory_space=pltpu.VMEM)
+    hbm = pl.BlockSpec(memory_space=pl.ANY)
+    sm = pl.BlockSpec(memory_space=pltpu.SMEM)
+    embed, grad_features, g, bias = pl.pallas_call(
+        layer_kernel,
+        out_shape=(
+            jax.ShapeDtypeStruct((1024, 256), BF),
+            jax.ShapeDtypeStruct((1024, 256), BF),
+            jax.ShapeDtypeStruct((768, 1024), BF),
+            jax.ShapeDtypeStruct((16, 128), F32),
+        ),
+        in_specs=[sm, hbm, hbm, hbm, hbm, vm, hbm, vm, hbm],
+        out_specs=(vm, vm, vm, vm),
+        scratch_shapes=LAYER_SCRATCH + AR_SCRATCH,
+        compiler_params=pltpu.CompilerParams(
+            collective_id=0, has_side_effects=True, vmem_limit_bytes=60 << 20
+        ),
+        name="layer",
+    )(
+        tile_cols, node_features, tile_weights, w_self, w_neigh,
+        bias_hidden.reshape(1, 1024), w_out, bias_out.reshape(1, 256), cotangent,
     )
-    activated, pullback = jax.vjp(gelu_tanh, preact)
-    hidden = activated.astype(jnp.bfloat16)
-    embed = (jnp.dot(hidden, w_out, preferred_element_type=jnp.float32) + bias_out).astype(
-        jnp.bfloat16
-    )
-    d_act = jnp.dot(cotangent, w_out.T, preferred_element_type=jnp.float32)
-    d_hidden = pullback(d_act)[0].astype(jnp.bfloat16)
-    partials = (
-        jnp.dot(node_features.T, d_hidden, preferred_element_type=jnp.float32),
-        jnp.dot(aggregate.T, d_hidden, preferred_element_type=jnp.float32),
-        jnp.sum(d_hidden.astype(jnp.float32), axis=0),
-        jnp.dot(cotangent.T, hidden, preferred_element_type=jnp.float32),
-        jnp.sum(cotangent.astype(jnp.float32), axis=0),
-    )
-    d_aggregate = jnp.dot(d_hidden, w_neigh.T, preferred_element_type=jnp.float32).astype(
-        jnp.bfloat16
-    )
-    d_self = jnp.dot(d_hidden, w_self.T, preferred_element_type=jnp.float32)
-    rim_total = adjoint_part(
-        adjacency, d_aggregate, local_idx, block_rows, tile_size, per_row, width
-    )
-    reduced = reduce_grads(partials)
-    grad_features = (d_self + rim_total).astype(jnp.bfloat16)
+    scale = 1.0 / math.sqrt(1024 * 256)
+    g = g.astype(F32) * scale
+    bias = bias.reshape(-1) * scale
     return (
-        embed,
-        grad_features,
-        reduced[0] * grad_scale,
-        reduced[1] * grad_scale,
-        reduced[2] * grad_scale,
-        reduced[3] * grad_scale,
-        reduced[4] * grad_scale,
+        embed, grad_features, g[:256], g[256:512], bias[:1024], g[512:].T, bias[1024:1280],
     )
 
 

time: 178 us -> 100 us (0.56)
  other arithmetic: 32.9 us -> 2.52 us
  matrix products: 29.7 us -> 0 us
  Pallas kernels: 69.2 us -> 89.6 us
  starting transfers between devices: 17.4 us -> 0 us
  waiting for transfers between devices: 15.6 us -> 0 us
  local copies, waits for them, and re-layouts: 11.9 us -> 6.95 us
    dot_general x11 -> x0, matrix products: 29.7 us -> none  [the longest x1 4.52 us: adjoint_part(): jnp.einsum('bij,bif->bjf', adjacency, d_aggregate.reshape(block_rows, til...]
    scatter-add x1 -> x0, other arithmetic: 26.5 us -> none  [adjoint_part(): spread_sum = spread_sum.at[local_idx.reshape(-1)].add(spread)]
    pallas_call x1, Pallas kernels: 69.2 us -> 89.6 us  [local(): pl.pallas_call(layer_kernel, out_shape=(jax.ShapeDtypeStruct((1024, 256),...]
    ppermute x4 -> x0, starting transfers between devices: 17.4 us -> none  [the longest x2 10.5 us: extended(): lax.ppermute(lax.slice_in_dim(block, 0, width, axis=dim), axis, backward)]
    ppermute x4 -> x0, waiting for transfers between devices: 15.6 us -> none  [the longest x2 11.1 us: extended(): lax.ppermute(lax.slice_in_dim(block, 0, width, axis=dim), axis, backward)]
    gather x1 -> x0, local copies, waits for them, and re-layouts: 2.78 us -> none  [local(): all_blocks[local_idx].reshape(block_rows, per_row * tile_size, width)]
    slice x1 -> x2, local copies, waits for them, and re-layouts: 3.77 us -> 1.16 us  [the longest x1 0.59 us: local(): bias[:1024]]
    broadcast_in_dim x3 -> x0, local copies, waits for them, and re-layouts: 2.18 us -> none  [the longest x1 2.09 us: adjoint_part(): spread_sum = jnp.zeros((3 * block_rows, tile_size, width), jnp.float32)]
  transfers between devices with their start and end apart: 4 -> 0, of which waited for: 2 -> 0; matrix products, arithmetic and copies ran while one was open for 9% -> 0% of each run, Pallas kernels for 39% -> 0%
where the time goes in v2:
time: 100 us; the launch traced here: 99.8 us
  Pallas kernels  89.6 us (90%)
  local copies, waits for them, and re-layouts  6.95 us (7%)
  other arithmetic  2.52 us (3%)
    pallas_call x1, Pallas kernels, local(): pl.pallas_call(layer_kernel, out_shape=(jax.ShapeDtypeStruct((1024, 256),...  89.6 us
    unnamed x8, local copies, waits for them, and re-layouts  4.26 us

profile of v2, /device:TPU:1, one launch (start us, length us, event | category | flops | bytes accessed | tf_op | source)
XLA Modules:
  0.0 99.8 jit_solution(2854750752241913301)
XLA Ops:
  0.6 1.4 %copy.16.cols = s32[16,8]{1,0:T(8,128)} copy(s32[16,8]{0,1:T(8,128)} %param.10) | data formatting | bytes 1024 | tf_op args[1]
  2.0 89.6 %layer.1 = (bf16[1024,256]{1,0:T(8,128)(2,1)}, bf16[1024,256]{1,0:T(8,128)(2,1)}, bf16[768,1024]{1,0:T(8,128)(2,1)}, f32[16,128]{1,0:T(8,128)}) custom-call(s32[16,8]{1,0:T(8,128)} %copy.16.cols, bf16[1024,256]{1,0:T(8,128)(2,1)} %x_hbm.1, s32[16,64,512]{2,1,0:T(8,128)} %tw_hbm.1, bf16[256,1024]{1,0:T(8,128)(2,1)} %ws_hbm.1, bf16[256,1024]{1,0:T(8,128)(2,1)} %wn_hbm.1, ...), custom_call_target="tpu_custom_call" | custom-call | tf_op jit(solution)/shard_map/layer/pallas_call | solution.py:456
  91.6 0.7 broadcast_multiply_fusion
  92.3 0.6 slice_bitcast_fusion.2
  92.9 0.6 slice_bitcast_fusion.1
  93.5 1.8 %convert_multiply_fusion = f32[768,1024]{1,0:T(8,128)S(1)} fusion(bf16[768,1024]{1,0:T(8,128)(2,1)} %get-tuple-element.13), kind=kLoop, calls=%fused_computation | loop fusion | flops 1572864 | bytes 4718592 | tf_op jit(solution)/shard_map/mul | solution.py:476
  95.3 0.0 copy-start.1
  95.3 1.5 %slice_bitcast_fusion = (f32[1024,256]{0,1:T(8,128)S(1)}, f32[256,1024]{1,0:T(8,128)}, f32[256,1024]{1,0:T(8,128)}) fusion(f32[768,1024]{1,0:T(8,128)S(1)} %convert_multiply_fusion), kind=kLoop, calls=%fused_computation.1 | loop fusion | bytes 6291456 | tf_op jit(solution)/shard_map/transpose | solution.py:479
  96.9 0.0 copy-start
  96.9 1.3 %copy.17 = f32[1024,256]{1,0:T(8,128)} copy(f32[1024,256]{0,1:T(8,128)S(1)} %get-tuple-element.22) | data formatting | bytes 2097152
  98.2 0.0 copy-done.1
  98.2 0.8 copy.20
  99.0 0.0 copy-done
  99.0 0.8 copy.21
Async XLA Ops:
  95.3 2.9 %copy-start.1 = (bf16[1024,256]{1,0:T(8,128)(2,1)S(1)}, bf16[1024,256]{1,0:T(8,128)(2,1)}, u32[]{:S(2)}) copy-start(bf16[1024,256]{1,0:T(8,128)(2,1)} %get-tuple-element.32) | copy-start | bytes 1572868
  96.9 2.1 %copy-start = (bf16[1024,256]{1,0:T(8,128)(2,1)S(1)}, bf16[1024,256]{1,0:T(8,128)(2,1)}, u32[]{:S(2)}) copy-start(bf16[1024,256]{1,0:T(8,128)(2,1)} %get-tuple-element.33) | copy-start | bytes 1572868

commit v3 on v2

--- a/solution.py
+++ b/solution.py
@@ -216,8 +216,8 @@
 def layer_kernel(
     cols, x_hbm, tw_hbm, ws_hbm, wn_hbm, bh, wo_hbm, bo, cot_hbm,
     embed, gradf, gout, bout,
-    win, tw, ws, wn, wo, cot, dup, dense, dense_t, pre, dact, agg0, agg, xt, ct, at,
-    hid, dh, dagg, bsum, own, lo, hi, lo_b, hi_b, from_r, from_l, g, bias,
+    win, tw, ws, wn, wo, cot, dup, dense, pre, dact, agg0, xt, ct, at,
+    hid, dh, da_t, bsum, own, lo, hi, lo_b, hi_b, from_r, from_l, g, bias,
     in_sem, halo_send, halo_recv, *ar,
 ):
     here, left, right = neighbours()
@@ -240,108 +240,87 @@
         c.start()
         halo.append(c)
 
-    for i in range(4):
-        far = pl.ds(256 * (3 - i), 256)
-        near = pl.ds(256 * i, 256)
-        halo_copy(x_hbm.at[far, :], win.at[far, :], 3 - i, right)
-        halo_copy(x_hbm.at[near, :], win.at[pl.ds(2048 + 256 * i, 256), :], 4 + i, left)
-
     def halo_wait(n):
         dst = win.at[pl.ds(256 * n if n < 4 else 1024 + 256 * n, 256), :]
         remote(dst, dst, halo_send.at[n], halo_recv.at[n], left).wait_recv()
 
-    loads[0].wait()
-    lane = lax.broadcasted_iota(jnp.int32, (64, 128), 1)
-    half = lax.broadcasted_iota(jnp.int32, (1, 128), 1) // 64
-
-    @pl.loop(0, 16)
-    def _(p):
-        c = p // 4
-        rows = pl.ds(pl.multiple_of((p % 4) * 64, 64), 64)
-        base = here * 16 - 16 + 4 * c
-        for q in range(4):
-            u = tw[p, :, 128 * q : 128 * q + 128].astype(F32) * SCALE_TILE
-            u = u.astype(BF).astype(F32)
-            r = pltpu.roll(u, 64, 1)
-            dup[2 * q] = jnp.where(lane < 64, u, r)
-            dup[2 * q + 1] = jnp.where(lane < 64, r, u)
-        spot = [cols[p, s] - base for s in range(8)]
-
-        @pl.loop(0, 18)
-        def _(j):
-            total = jnp.zeros((64, 128), F32)
-            for s in range(8):
-                hit = jnp.where(half == spot[s] - 2 * j, 1.0, 0.0).astype(F32)
-                total = total + dup[s] * hit
-            dense[c, rows, pl.ds(pl.multiple_of(j * 128, 128), 128)] = total.astype(BF)
-
-    @pl.loop(0, 36)
-    def _(i):
-        c, t = i // 9, i % 9
-        dense_t[c, ds256(t), :] = dense[c, :, ds256(t)].T
-
-    for c in loads[1:]:
-        c.wait()
-
-    bsum[...] = jnp.zeros_like(bsum)
-
-    @pl.loop(0, 4)
-    def _(c):
-        rows = ds256(c)
-        mine = pl.ds(pl.multiple_of(1024 + c * 256, 256), 256)
-        xc = win[mine, :]
-        cc = cot[rows, :]
-        xt[:, rows] = xc.T
-        ct[:, rows] = cc.T
-        bsum[:, 1024:1280] += jnp.sum(cc.astype(F32).reshape(32, 8, 256), axis=0)
+    for i in range(4):
+        rows = pl.ds(256 * i, 256)
+        halo_copy(x_hbm.at[rows, :], win.at[rows, :], i, right)
+    for i in range(4):
+        rows = pl.ds(256 * i, 256)
+        halo_copy(x_hbm.at[rows, :], win.at[pl.ds(2048 + 256 * i, 256), :], 4 + i, left)
+
+    def build_dense():
+        lane = lax.broadcasted_iota(jnp.int32, (64, 128), 1)
+        half = lax.broadcasted_iota(jnp.int32, (1, 128), 1) // 64
+
+        @pl.loop(0, 16)
+        def _(p):
+            c = p // 4
+            rows = pl.ds(pl.multiple_of((p % 4) * 64, 64), 64)
+            base = here * 16 - 16 + 4 * c
+            for q in range(4):
+                u = tw[p, :, 128 * q : 128 * q + 128].astype(F32) * SCALE_TILE
+                u = u.astype(BF).astype(F32)
+                r = pltpu.roll(u, 64, 1)
+                dup[2 * q] = jnp.where(lane < 64, u, r)
+                dup[2 * q + 1] = jnp.where(lane < 64, r, u)
+            spot = [cols[s, p] - base for s in range(8)]
+
+            @pl.loop(0, 18)
+            def _(j):
+                total = jnp.zeros((64, 128), F32)
+                for s in range(8):
+                    hit = jnp.where(half == spot[s] - 2 * j, 1.0, 0.0).astype(F32)
+                    total = total + dup[s] * hit
+                dense[c, rows, pl.ds(pl.multiple_of(j * 128, 128), 128)] = total.astype(BF)
+
+    def local_part():
+        bsum[...] = jnp.zeros_like(bsum)
+
+        @pl.loop(0, 4)
+        def _(c):
+            rows = ds256(c)
+            mine = pl.ds(pl.multiple_of(1024 + c * 256, 256), 256)
+            xc = win[mine, :]
+            cc = cot[rows, :]
+            xt[:, rows] = xc.T
+            ct[:, rows] = cc.T
+            bsum[:, 1024:1280] += jnp.sum(cc.astype(F32).reshape(32, 8, 256), axis=0)
+            for n in range(4):
+                n4 = slice(256 * n, 256 * n + 256)
+                pre[rows, n4] = mm(xc, ws[:, n4]) + bh[:, n4]
+                dact[rows, n4] = mm_t(cc, wo[n4, :])
+            total = jnp.zeros((256, 256), F32)
+            for t in range(4):
+                total = total + mm(dense[c, :, ds256(4 + t - c)], win[1024 + 256 * t : 1280 + 256 * t, :])
+            agg0[rows, :] = total
+
+    def low_part():
+        for c in range(4):
+            rows = slice(256 * c, 256 * c + 256)
+            total = agg0[rows, :]
+            for t in range(c, 4):
+                total = total + mm(dense[c, :, 256 * (t - c) : 256 * (t - c) + 256], win[256 * t : 256 * t + 256, :])
+            agg0[rows, :] = total
+
+    def adjoint_send(n, buf, src, dst, dev):
+        j = n % 4
+        buf[j] = src[:, 256 * j : 256 * j + 256].astype(BF)
+        halo_copy(buf.at[j], dst.at[j], 8 + n, dev)
+
+    def chunk(c):
+        r4 = slice(256 * c, 256 * c + 256)
+        total = agg0[r4, :]
+        for t in range(c + 1):
+            b = 256 * (8 + t - c)
+            total = total + mm(dense[c, :, b : b + 256], win[2048 + 256 * t : 2304 + 256 * t, :])
+        ag = total.astype(BF)
         for n in range(4):
             n4 = slice(256 * n, 256 * n + 256)
-            pre[rows, n4] = mm(xc, ws[:, n4]) + bh[:, n4]
-            dact[rows, n4] = mm_t(cc, wo[n4, :])
-        total = jnp.zeros((256, 256), F32)
-        for t in range(4):
-            total = total + mm(dense[c, :, ds256(4 + t - c)], win[1024 + 256 * t : 1280 + 256 * t, :])
-        agg0[rows, :] = total
-
-    lo[...] = jnp.zeros_like(lo)
-    hi[...] = jnp.zeros_like(hi)
-
-    def adjoint_send(n, buf, src, dst, dev):
-        piece = pl.ds(256 * (n % 4), 256)
-        buf[piece, :] = src[piece, :].astype(BF)
-        halo_copy(buf.at[piece, :], dst.at[piece, :], 8 + n, dev)
-
-    @pl.loop(0, 4)
-    def _(k):
-        c = (k + 1) % 3 + 2 * (k // 3)
-
-        @pl.when(k == 0)
-        def _():
-            for n in (3, 4, 2, 5, 1):
-                halo_wait(n)
-
-        @pl.when(k == 1)
-        def _():
-            halo_wait(6)
-
-        @pl.when(k == 2)
-        def _():
-            halo_wait(0)
-
-        @pl.when(k == 3)
-        def _():
-            halo_wait(7)
-
-        rows = ds256(c)
-        total = agg0[rows, :]
-        for t in range(5):
-            w = c + t + 4 * ((c + t) // 4)
-            total = total + mm(dense[c, :, ds256(w - c)], win[ds256(w), :])
-        ag = total.astype(BF)
-        agg[rows, :] = ag
-        for n in range(4):
-            n4 = slice(256 * n, 256 * n + 256)
-            pre[rows, n4] += mm(ag, wn[:, n4])
+            pre[r4, n4] += mm(ag, wn[:, n4])
+        at[:, r4] = ag.T
 
         @pl.loop(0, 8)
         def _(i):
@@ -350,63 +329,73 @@
                 n4 = slice(256 * n, 256 * n + 256)
                 v = pre[r, n4]
                 u = v * v
-                th = jnp.tanh(v * (C0 + C1 * u))
-                a = 0.5 * th + 0.5
-                hid[r, n4] = (v * a).astype(BF)
-                slope = a + (0.5 * v) * (1.0 - th * th) * (C0 + (3.0 * C1) * u)
+                a = 0.5 * jnp.tanh(v * (C0 + C1 * u)) + 0.5
+                h = v * a
+                hid[r, n4] = h.astype(BF)
+                slope = a + h * ((2.0 * C0) + (6.0 * C1) * u) * (1.0 - a)
                 d = (dact[r, n4] * slope).astype(BF)
                 dh[r, n4] = d
                 bsum[:, n4] += jnp.sum(d.astype(F32).reshape(4, 8, 256), axis=0)
 
-        da = mm_t(dh[rows, :], wn[...]).astype(BF)
-        dagg[rows, :] = da
-        for t in range(4):
-            @pl.when(c + t < 4)
-            def _():
-                lo[ds256(c + t), :] += mm(dense_t[c, ds256(t), :], da)
-
-            @pl.when(t <= c)
-            def _():
-                hi[pl.ds(256 * t, 256), :] += mm(dense_t[c, ds256(8 - c + t), :], da)
-
-    for n in (3, 2, 1, 0):
-        adjoint_send(4 + n, hi_b, hi, from_l, right)
-        adjoint_send(3 - n, lo_b, lo, from_r, left)
-
-    for c in range(4):
-        at[:, 256 * c : 256 * c + 256] = agg[256 * c : 256 * c + 256, :].T
-    for n in range(4):
-        n4 = slice(256 * n, 256 * n + 256)
-        g[0:256, n4] = mm(xt[...], dh[:, n4]).astype(BF)
-        g[256:512, n4] = mm(at[...], dh[:, n4]).astype(BF)
-        g[512:768, n4] = mm(ct[...], hid[:, n4]).astype(BF)
-    sums = jnp.sum(bsum[...], axis=0, keepdims=True)
-    for n in range(10):
-        bias[n : n + 1, :] = sums[:, 128 * n : 128 * n + 128]
-    bias[10:16, :] = jnp.zeros((6, 128), F32)
+        da = mm_t(wn[...], dh[r4, :]).astype(BF)
+        da_t[c] = da
+        for j in range(c, 4):
+            part = mm(da, dense[c, :, 256 * (j - c) : 256 * (j - c) + 256])
+            j4 = slice(256 * j, 256 * j + 256)
+            lo[:, j4] = part if c == 0 else lo[:, j4] + part
+            if j == c:
+                adjoint_send(j, lo_b, lo, from_r, left)
+        for j in range(c + 1):
+            b = 256 * (8 + j - c)
+            part = mm(da, dense[c, :, b : b + 256])
+            j4 = slice(256 * j, 256 * j + 256)
+            hi[:, j4] = part if c == j else hi[:, j4] + part
+            if c == 3:
+                adjoint_send(4 + j, hi_b, hi, from_l, right)
+
+    def weight_grads():
+        for n in range(4):
+            n4 = slice(256 * n, 256 * n + 256)
+            g[0:256, n4] = mm(xt[...], dh[:, n4]).astype(BF)
+            g[256:512, n4] = mm(at[...], dh[:, n4]).astype(BF)
+            g[512:768, n4] = mm(ct[...], hid[:, n4]).astype(BF)
+        sums = jnp.sum(bsum[...], axis=0, keepdims=True)
+        for n in range(10):
+            bias[n : n + 1, :] = sums[:, 128 * n : 128 * n + 128]
+        bias[10:16, :] = jnp.zeros((6, 128), F32)
 
     def local_rest():
         @pl.loop(0, 4)
         def _(c):
             rows = ds256(c)
             embed[rows, :] = (mm(hid[rows, :], wo[...]) + bo[...]).astype(BF)
-            total = mm_t(dh[rows, :], ws[...])
+            total = jnp.zeros((256, 256), F32)
             for b in range(4):
-                total = total + mm(dense_t[b, ds256(4 + c - b), :], dagg[256 * b : 256 * b + 256, :])
-            own[rows, :] = total
-
+                total = total + mm(da_t[b], dense[b, :, ds256(4 + c - b)])
+            own[rows, :] = mm_t(dh[rows, :], ws[...]) + total.T
+
+    def last_sum():
+        for j in (0, 1, 2, 3):
+            for m, dst in ((j, from_r), (4 + j, from_l)):
+                remote(dst.at[j], dst.at[j], halo_send.at[8 + m], halo_recv.at[8 + m], left).wait_recv()
+            rows = slice(256 * j, 256 * j + 256)
+            outer = from_l[j].astype(F32) + from_r[j].astype(F32)
+            gradf[rows, :] = (own[rows, :] + outer.T).astype(BF)
+
+    loads[0].wait()
+    build_dense()
+    for c in loads[1:]:
+        c.wait()
+    local_part()
+    for n in range(4):
+        halo_wait(n)
+    low_part()
+    for c in range(4):
+        halo_wait(4 + c)
+        chunk(c)
+    weight_grads()
     reduce_all(g, bias, gout, bout, *ar, hook=local_rest)
-
-    for n in (3, 2, 1, 0):
-        for m, dst in ((4 + n, from_l), (3 - n, from_r)):
-            piece = dst.at[pl.ds(256 * (m % 4), 256), :]
-            remote(piece, piece, halo_send.at[8 + m], halo_recv.at[8 + m], left).wait_recv()
-
-    @pl.loop(0, 16)
-    def _(i):
-        r = pl.ds(pl.multiple_of(i * 64, 64), 64)
-        gradf[r, :] = (own[r, :] + from_l[r, :].astype(F32) + from_r[r, :].astype(F32)).astype(BF)
-
+    last_sum()
     for c in halo:
         c.wait_send()
 
@@ -420,25 +409,23 @@
     pltpu.VMEM((1024, 256), BF),
     pltpu.VMEM((8, 64, 128), F32),
     pltpu.VMEM((4, 256, 2304), BF),
-    pltpu.VMEM((4, 2304, 256), BF),
     pltpu.VMEM((1024, 1024), F32),
     pltpu.VMEM((1024, 1024), F32),
     pltpu.VMEM((1024, 256), F32),
-    pltpu.VMEM((1024, 256), BF),
     pltpu.VMEM((256, 1024), BF),
     pltpu.VMEM((256, 1024), BF),
     pltpu.VMEM((256, 1024), BF),
     pltpu.VMEM((1024, 1024), BF),
     pltpu.VMEM((1024, 1024), BF),
-    pltpu.VMEM((1024, 256), BF),
+    pltpu.VMEM((4, 256, 256), BF),
     pltpu.VMEM((8, 1280), F32),
     pltpu.VMEM((1024, 256), F32),
-    pltpu.VMEM((1024, 256), F32),
-    pltpu.VMEM((1024, 256), F32),
-    pltpu.VMEM((1024, 256), BF),
-    pltpu.VMEM((1024, 256), BF),
-    pltpu.VMEM((1024, 256), BF),
-    pltpu.VMEM((1024, 256), BF),
+    pltpu.VMEM((256, 1024), F32),
+    pltpu.VMEM((256, 1024), F32),
+    pltpu.VMEM((4, 256, 256), BF),
+    pltpu.VMEM((4, 256, 256), BF),
+    pltpu.VMEM((4, 256, 256), BF),
+    pltpu.VMEM((4, 256, 256), BF),
     pltpu.VMEM((768, 1024), BF),
     pltpu.VMEM((16, 128), F32),
     pltpu.SemaphoreType.DMA((6,)),
@@ -469,7 +456,7 @@
         ),
         name="layer",
     )(
-        tile_cols, node_features, tile_weights, w_self, w_neigh,
+        tile_cols.T, node_features, tile_weights, w_self, w_neigh,
         bias_hidden.reshape(1, 1024), w_out, bias_out.reshape(1, 256), cotangent,
     )
     scale = 1.0 / math.sqrt(1024 * 256)

time: 100 us -> 92.8 us (0.928)
  Pallas kernels: 89.6 us -> 83.8 us
  local copies, waits for them, and re-layouts: 6.95 us -> 5.59 us
    pallas_call x1, Pallas kernels: 89.6 us -> 83.8 us  [local(): pl.pallas_call(layer_kernel, out_shape=(jax.ShapeDtypeStruct((1024, 256),...]
    unnamed x8 -> x7, local copies, waits for them, and re-layouts: 4.26 us -> 2.9 us
where the time goes in v3:
time: 92.8 us; the launch traced here: 92.6 us
  Pallas kernels  83.8 us (90%)
  local copies, waits for them, and re-layouts  5.59 us (6%)
  other arithmetic  2.52 us (3%)
    pallas_call x1, Pallas kernels, local(): pl.pallas_call(layer_kernel, out_shape=(jax.ShapeDtypeStruct((1024, 256),...  83.8 us
    unnamed x7, local copies, waits for them, and re-layouts  2.9 us

profile of v3, /device:TPU:1, one launch (start us, length us, event | category | flops | bytes accessed | tf_op | source)
XLA Modules:
  0.0 92.6 jit_solution(5384765585733199481)
XLA Ops:
  0.6 83.8 %layer.1 = (bf16[1024,256]{1,0:T(8,128)(2,1)}, bf16[1024,256]{1,0:T(8,128)(2,1)}, bf16[768,1024]{1,0:T(8,128)(2,1)}, f32[16,128]{1,0:T(8,128)}) custom-call(s32[8,16]{1,0:T(8,128)} %bitcast.9, bf16[1024,256]{1,0:T(8,128)(2,1)} %x_hbm.1, s32[16,64,512]{2,1,0:T(8,128)} %tw_hbm.1, bf16[256,1024]{1,0:T(8,128)(2,1)} %ws_hbm.1, bf16[256,1024]{1,0:T(8,128)(2,1)} %wn_hbm.1, ...), custom_call_target="tpu_custom_call" | custom-call | tf_op jit(solution)/shard_map/layer/pallas_call | solution.py:443
  84.5 0.7 broadcast_multiply_fusion
  85.2 0.6 slice_bitcast_fusion.2
  85.7 0.6 slice_bitcast_fusion.1
  86.3 1.8 %convert_multiply_fusion = f32[768,1024]{1,0:T(8,128)S(1)} fusion(bf16[768,1024]{1,0:T(8,128)(2,1)} %get-tuple-element.13), kind=kLoop, calls=%fused_computation | loop fusion | flops 1572864 | bytes 4718592 | tf_op jit(solution)/shard_map/mul | solution.py:463
  88.2 0.0 copy-start.1
  88.2 1.5 %slice_bitcast_fusion = (f32[1024,256]{0,1:T(8,128)S(1)}, f32[256,1024]{1,0:T(8,128)}, f32[256,1024]{1,0:T(8,128)}) fusion(f32[768,1024]{1,0:T(8,128)S(1)} %convert_multiply_fusion), kind=kLoop, calls=%fused_computation.1 | loop fusion | bytes 6291456 | tf_op jit(solution)/shard_map/transpose | solution.py:466
  89.7 0.0 copy-start
  89.7 1.3 %copy.16 = f32[1024,256]{1,0:T(8,128)} copy(f32[1024,256]{0,1:T(8,128)S(1)} %get-tuple-element.22) | data formatting | bytes 2097152
  91.0 0.0 copy-done.1
  91.0 0.8 copy.19
  91.8 0.0 copy-done
  91.8 0.8 copy.20
Async XLA Ops:
  88.2 2.9 %copy-start.1 = (bf16[1024,256]{1,0:T(8,128)(2,1)S(1)}, bf16[1024,256]{1,0:T(8,128)(2,1)}, u32[]{:S(2)}) copy-start(bf16[1024,256]{1,0:T(8,128)(2,1)} %get-tuple-element.32) | copy-start | bytes 1572868
  89.7 2.1 %copy-start = (bf16[1024,256]{1,0:T(8,128)(2,1)S(1)}, bf16[1024,256]{1,0:T(8,128)(2,1)}, u32[]{:S(2)}) copy-start(bf16[1024,256]{1,0:T(8,128)(2,1)} %get-tuple-element.33) | copy-start | bytes 1572868

commit v4 on v3

--- a/solution.py
+++ b/solution.py
@@ -38,17 +38,26 @@
         device_id=(dev[0], dev[1]), device_id_type=MESH)
 
 
-def reduce_all(g, bias, gout, bout, rc, s1, r1, t1, r2, zin, rz, zc, zfull, bc, bx, by, bz,
-               send, recv, hook=None):
+BATCH, HALF, PART = 256, 128, 32
+
+
+def line_sum(own, line, at):
+    total = own
+    for dev in line:
+        total = total + at(dev[2]).astype(F32)
+    return total
+
+
+def make_reduce(g, bias, gout, bout, rc, s1, r1, t1, r2, zin, rz, zfull, bc, bx, by, bz,
+                send, recv):
     row, z_lo, core, x, y, z = coords()
     sibling, xs, ys, zs = partners()
-    A, B = 384, 96
+    first = ((xs, x), (ys, y))
+    second = ((ys, y), (xs, x))
     sent = []
-    nsend = [0]
 
     def go(src, dst, rsem, dev):
-        c = remote(src, dst, send.at[nsend[0]], recv.at[rsem], dev)
-        nsend[0] += 1
+        c = remote(src, dst, send.at[len(sent)], recv.at[rsem], dev)
         c.start()
         sent.append(c)
 
@@ -57,126 +66,169 @@
 
     mine = pl.ds(pl.multiple_of(core * 512, 512), 512)
     other = pl.ds(pl.multiple_of((1 - core) * 512, 512), 512)
-    go(g.at[:, other], rc, 0, sibling[0])
-    go(bias, bc, 1, sibling[0])
-    if hook is not None:
-        hook()
-    land(rc, 0)
-    land(bc, 1)
-
-    @pl.loop(0, 8)
-    def _(i):
-        rows = pl.ds(pl.multiple_of(i * 96, 96), 96)
-        s1[rows, :] = (g[rows, mine].astype(F32) + rc[rows, :].astype(F32)).astype(BF)
-
-    b1 = bias[...] + bc[...]
-    bx[x] = b1
-    base = 2
-    for h, (line, me) in enumerate(((xs, x), (ys, y))):
-        for dev in line:
-            j = dev[2]
-            rows = pl.ds(pl.multiple_of(h * A + j * B, B), B)
-            go(s1.at[rows, :], r1.at[h, me], base + h * 4 + me, dev)
-    for dev in xs:
-        go(bx.at[x], bx.at[x], base + 8 + x, dev)
-    for h, (line, me) in enumerate(((xs, x), (ys, y))):
-        for dev in line:
-            land(r1.at[h, dev[2]], base + h * 4 + dev[2])
-        own = pl.ds(pl.multiple_of(h * A + me * B, B), B)
-        total = s1[own, :].astype(F32)
-        for dev in line:
-            total = total + r1[h, dev[2]].astype(F32)
-        t1[h] = total.astype(BF)
-    for dev in xs:
-        land(bx.at[dev[2]], base + 8 + dev[2])
-    by[y] = bx[0] + bx[1] + bx[2] + bx[3]
-    base = 14
-    for h, (line, me) in enumerate(((ys, y), (xs, x))):
-        for dev in line:
-            lanes = pl.ds(pl.multiple_of(dev[2] * 128, 128), 128)
-            go(t1.at[h, :, lanes], r2.at[h, me], base + h * 4 + me, dev)
-    for dev in ys:
-        go(by.at[y], by.at[y], base + 8 + y, dev)
-    for h, (line, me) in enumerate(((ys, y), (xs, x))):
-        for dev in line:
-            land(r2.at[h, dev[2]], base + h * 4 + dev[2])
-        total = t1[h, :, pl.ds(pl.multiple_of(me * 128, 128), 128)].astype(F32)
-        for dev in line:
-            total = total + r2[h, dev[2]].astype(F32)
-        zin[h * 4 : h * 4 + 4] = total.reshape(4, 24, 128)
-    for dev in ys:
-        land(by.at[dev[2]], base + 8 + dev[2])
-    bz[z] = by[0] + by[1] + by[2] + by[3]
-    base = 26
-    for dev in zs:
-        go(zin.at[dev[2]], rz.at[z], base + z, dev)
-    for dev in zs:
-        go(bz.at[z], bz.at[z], base + 8 + z, dev)
-    total = zin[z]
-    for dev in zs:
-        land(rz.at[dev[2]], base + dev[2])
-        total = total + rz[dev[2]]
-    zfull[z] = total
-    base = 42
-    for dev in zs:
-        go(zfull.at[z], zfull.at[z], base + z, dev)
-    for dev in zs:
-        land(bz.at[dev[2]], 34 + dev[2])
-    bout[...] = (((bz[0] + bz[1]) + (bz[2] + bz[3])) + ((bz[4] + bz[5]) + (bz[6] + bz[7])))
-    for dev in zs:
-        land(zfull.at[dev[2]], base + dev[2])
-    base = 50
-    for h, (own, line, me) in enumerate(((x, ys, y), (y, xs, x))):
-        rows = pl.ds(pl.multiple_of(h * A + own * B, B), B)
-        lane0 = core * 512
-
-        def at(j):
-            return pl.ds(pl.multiple_of(lane0 + j * 128, 128), 128)
-
-        gout[rows, at(me)] = zfull[h * 4 : h * 4 + 4].reshape(96, 128).astype(BF)
-        for dev in line:
-            go(gout.at[rows, at(me)], gout.at[rows, at(me)], base + h * 4 + me, dev)
-    for h, (own, line, me) in enumerate(((x, ys, y), (y, xs, x))):
-        rows = pl.ds(pl.multiple_of(h * A + own * B, B), B)
-        lane0 = core * 512
-        for dev in line:
-            piece = gout.at[rows, pl.ds(pl.multiple_of(lane0 + dev[2] * 128, 128), 128)]
-            land(piece, base + h * 4 + dev[2])
-    base = 58
-    for h, (line, me) in enumerate(((xs, x), (ys, y))):
-        rows = pl.ds(pl.multiple_of(h * A + me * B, B), B)
-        for dev in line:
-            go(gout.at[rows, mine], gout.at[rows, mine], base + h * 4 + me, dev)
-        go(gout.at[rows, mine], gout.at[rows, mine], 66 + h * 4 + me, sibling[0])
-    for h, (line, me) in enumerate(((xs, x), (ys, y))):
-        for dev in line:
-            rows = pl.ds(pl.multiple_of(h * A + dev[2] * B, B), B)
-            land(gout.at[rows, mine], base + h * 4 + dev[2])
-            go(gout.at[rows, mine], gout.at[rows, mine], 66 + h * 4 + dev[2], sibling[0])
-    for h in range(2):
-        for j in range(4):
-            rows = pl.ds(h * A + j * B, B)
-            land(gout.at[rows, other], 66 + h * 4 + j)
-    for c in sent:
-        c.wait_send()
+
+    def batch(b):
+        return pl.ds(b * BATCH, BATCH)
+
+    def part(b, h, j):
+        return pl.ds(pl.multiple_of(b * BATCH + h * HALF + j * PART, PART), PART)
+
+    def block(j):
+        return pl.ds(pl.multiple_of(core * 512 + j * 128, 128), 128)
+
+    def n_core(b):
+        return b
+
+    def n_s1(b, h, j):
+        return 3 + b * 8 + h * 4 + j
+
+    def n_s2(b, h, j):
+        return 27 + b * 8 + h * 4 + j
+
+    def n_z(b, j):
+        return 51 + b * 8 + j
+
+    def n_zback(b, j):
+        return 75 + b * 8 + j
+
+    def n_s2back(b, h, j):
+        return 99 + b * 8 + h * 4 + j
+
+    def n_s1back(b, h, j):
+        return 123 + b * 8 + h * 4 + j
+
+    def n_coreback(b, h, j):
+        return 147 + b * 8 + h * 4 + j
+
+    n_bias = 171
+
+    def pair(b):
+        go(g.at[batch(b), other], rc.at[batch(b), :], n_core(b), sibling[0])
+
+    def pair_bias():
+        go(bias, bc, n_bias, sibling[0])
+
+    def over_first(b):
+        land(rc.at[batch(b), :], n_core(b))
+        for h, (line, me) in enumerate(first):
+            s1[pl.ds(b * BATCH + h * HALF, HALF), :] = (
+                g[pl.ds(b * BATCH + h * HALF, HALF), mine].astype(F32)
+                + rc[pl.ds(b * BATCH + h * HALF, HALF), :].astype(F32)
+            ).astype(BF)
+        for n in range(3):
+            for h, (line, me) in enumerate(first):
+                dev = line[n]
+                go(s1.at[part(b, h, dev[2]), :], r1.at[b, h, me], n_s1(b, h, me), dev)
+
+    def bias_first():
+        land(bc, n_bias)
+        bx[x] = bias[...] + bc[...]
+        for dev in xs:
+            go(bx.at[x], bx.at[x], n_bias + 1 + x, dev)
+
+    def over_second(b):
+        for h, (line, me) in enumerate(first):
+            for dev in line:
+                land(r1.at[b, h, dev[2]], n_s1(b, h, dev[2]))
+            total = line_sum(s1[part(b, h, me), :].astype(F32), line, lambda j: r1[b, h, j])
+            t1[b, h] = total.astype(BF)
+            for dev in second[h][0]:
+                lanes = pl.ds(pl.multiple_of(dev[2] * 128, 128), 128)
+                m = second[h][1]
+                go(t1.at[b, h, :, lanes], r2.at[b, h, m], n_s2(b, h, m), dev)
+
+    def bias_second():
+        for dev in xs:
+            land(bx.at[dev[2]], n_bias + 1 + dev[2])
+        by[y] = bx[0] + bx[1] + bx[2] + bx[3]
+        for dev in ys:
+            go(by.at[y], by.at[y], n_bias + 5 + y, dev)
+
+    def over_z(b):
+        for h, (line, me) in enumerate(second):
+            for dev in line:
+                land(r2.at[b, h, dev[2]], n_s2(b, h, dev[2]))
+            own = t1[b, h, :, pl.ds(pl.multiple_of(me * 128, 128), 128)].astype(F32)
+            total = line_sum(own, line, lambda j: r2[b, h, j])
+            zin[b, h * 4 : h * 4 + 4] = total.reshape(4, 8, 128)
+        for dev in zs:
+            go(zin.at[b, dev[2]], rz.at[b, z], n_z(b, z), dev)
+
+    def bias_z():
+        for dev in ys:
+            land(by.at[dev[2]], n_bias + 5 + dev[2])
+        bz[z] = by[0] + by[1] + by[2] + by[3]
+        for dev in zs:
+            go(bz.at[z], bz.at[z], n_bias + 9 + z, dev)
+
+    def back_z(b):
+        for dev in zs:
+            land(rz.at[b, dev[2]], n_z(b, dev[2]))
+        zfull[b, z] = line_sum(zin[b, z], zs, lambda j: rz[b, j])
+        for dev in zs:
+            go(zfull.at[b, z], zfull.at[b, z], n_zback(b, z), dev)
+
+    def bias_end():
+        for dev in zs:
+            land(bz.at[dev[2]], n_bias + 9 + dev[2])
+        bout[...] = ((bz[0] + bz[1]) + (bz[2] + bz[3])) + ((bz[4] + bz[5]) + (bz[6] + bz[7]))
+
+    def back_second(b):
+        for dev in zs:
+            land(zfull.at[b, dev[2]], n_zback(b, dev[2]))
+        for h, (line, me) in enumerate(second):
+            rows = part(b, h, first[h][1])
+            gout[rows, block(me)] = zfull[b, h * 4 : h * 4 + 4].reshape(PART, 128).astype(BF)
+            for dev in line:
+                go(gout.at[rows, block(me)], gout.at[rows, block(me)], n_s2back(b, h, me), dev)
+
+    def back_first(b):
+        for h, (line, me) in enumerate(second):
+            own = first[h][1]
+            rows = part(b, h, own)
+            for dev in line:
+                land(gout.at[rows, block(dev[2])], n_s2back(b, h, dev[2]))
+            for dev in first[h][0]:
+                go(gout.at[rows, mine], gout.at[rows, mine], n_s1back(b, h, own), dev)
+            go(gout.at[rows, mine], gout.at[rows, mine], n_coreback(b, h, own), sibling[0])
+
+    def back_pair(b):
+        for h, (line, me) in enumerate(first):
+            for dev in line:
+                rows = part(b, h, dev[2])
+                land(gout.at[rows, mine], n_s1back(b, h, dev[2]))
+                go(gout.at[rows, mine], gout.at[rows, mine], n_coreback(b, h, dev[2]), sibling[0])
+
+    def back_end(b):
+        for h in range(2):
+            for j in range(4):
+                land(gout.at[part(b, h, j), other], n_coreback(b, h, j))
+
+    def finish():
+        for c in sent:
+            c.wait_send()
+
+    return dict(pair=pair, pair_bias=pair_bias, over_first=over_first, bias_first=bias_first,
+                over_second=over_second, bias_second=bias_second, over_z=over_z, bias_z=bias_z,
+                back_z=back_z, bias_end=bias_end, back_second=back_second, back_first=back_first,
+                back_pair=back_pair, back_end=back_end, finish=finish)
 
 
 AR_SCRATCH = [
     pltpu.VMEM((768, 512), BF),
     pltpu.VMEM((768, 512), BF),
-    pltpu.VMEM((2, 4, 96, 512), BF),
-    pltpu.VMEM((2, 96, 512), BF),
-    pltpu.VMEM((2, 4, 96, 128), BF),
-    pltpu.VMEM((8, 24, 128), F32),
-    pltpu.VMEM((8, 24, 128), F32),
-    pltpu.VMEM((24, 128), F32),
-    pltpu.VMEM((8, 24, 128), F32),
+    pltpu.VMEM((3, 2, 4, 32, 512), BF),
+    pltpu.VMEM((3, 2, 32, 512), BF),
+    pltpu.VMEM((3, 2, 4, 32, 128), BF),
+    pltpu.VMEM((3, 8, 8, 128), F32),
+    pltpu.VMEM((3, 8, 8, 128), F32),
+    pltpu.VMEM((3, 8, 8, 128), F32),
     pltpu.VMEM((16, 128), F32),
     pltpu.VMEM((4, 16, 128), F32),
     pltpu.VMEM((4, 16, 128), F32),
     pltpu.VMEM((8, 16, 128), F32),
-    pltpu.SemaphoreType.DMA((80,)),
-    pltpu.SemaphoreType.DMA((80,)),
+    pltpu.SemaphoreType.DMA((184,)),
+    pltpu.SemaphoreType.DMA((192,)),
 ]
 
 
@@ -203,6 +255,9 @@
 
 def ds256(i):
     return pl.ds(pl.multiple_of(i * 256, 256), 256)
+
+
+SENDS = {0: (0,), 1: (1,), 2: (2,), 3: (7, 3, 6), "back_z": (5, 4)}
 
 
 def neighbours():
@@ -215,10 +270,11 @@
 
 def layer_kernel(
     cols, x_hbm, tw_hbm, ws_hbm, wn_hbm, bh, wo_hbm, bo, cot_hbm,
-    embed, gradf, gout, bout,
+    embed_hbm, gradf_hbm, gwo_hbm, gws_hbm, gwn_hbm, bout,
+    embed, gradf, gout, gwo,
     win, tw, ws, wn, wo, cot, dup, dense, pre, dact, agg0, xt, ct, at,
     hid, dh, da_t, bsum, own, lo, hi, lo_b, hi_b, from_r, from_l, g, bias,
-    in_sem, halo_send, halo_recv, *ar,
+    in_sem, out_sem, halo_send, halo_recv, *ar,
 ):
     here, left, right = neighbours()
     sibling, xs, ys, zs = partners()
@@ -234,6 +290,12 @@
     greet([left, right] + sibling + xs + ys + zs)
 
     halo = []
+    writes = []
+
+    def write(src, dst):
+        c = pltpu.make_async_copy(src, dst, out_sem.at[len(writes)])
+        c.start()
+        writes.append(c)
 
     def halo_copy(src, dst, n, dev):
         c = remote(src, dst, halo_send.at[n], halo_recv.at[n], dev)
@@ -305,10 +367,16 @@
                 total = total + mm(dense[c, :, 256 * (t - c) : 256 * (t - c) + 256], win[256 * t : 256 * t + 256, :])
             agg0[rows, :] = total
 
-    def adjoint_send(n, buf, src, dst, dev):
+    def adjoint_round(n):
         j = n % 4
+        src, buf = ((lo, lo_b), (hi, hi_b))[n // 4]
         buf[j] = src[:, 256 * j : 256 * j + 256].astype(BF)
-        halo_copy(buf.at[j], dst.at[j], 8 + n, dev)
+
+    def adjoint_send(pieces):
+        for n in pieces:
+            j = n % 4
+            buf, dst, dev = ((lo_b, from_r, left), (hi_b, from_l, right))[n // 4]
+            halo_copy(buf.at[j], dst.at[j], 8 + n, dev)
 
     def chunk(c):
         r4 = slice(256 * c, 256 * c + 256)
@@ -344,21 +412,22 @@
             j4 = slice(256 * j, 256 * j + 256)
             lo[:, j4] = part if c == 0 else lo[:, j4] + part
             if j == c:
-                adjoint_send(j, lo_b, lo, from_r, left)
+                adjoint_round(j)
         for j in range(c + 1):
             b = 256 * (8 + j - c)
             part = mm(da, dense[c, :, b : b + 256])
             j4 = slice(256 * j, 256 * j + 256)
             hi[:, j4] = part if c == j else hi[:, j4] + part
             if c == 3:
-                adjoint_send(4 + j, hi_b, hi, from_l, right)
-
-    def weight_grads():
+                adjoint_round(4 + j)
+
+    def weight_grad(b):
+        left_side, right_side = ((ct, hid), (xt, dh), (at, dh))[b]
         for n in range(4):
             n4 = slice(256 * n, 256 * n + 256)
-            g[0:256, n4] = mm(xt[...], dh[:, n4]).astype(BF)
-            g[256:512, n4] = mm(at[...], dh[:, n4]).astype(BF)
-            g[512:768, n4] = mm(ct[...], hid[:, n4]).astype(BF)
+            g[256 * b : 256 * b + 256, n4] = mm(left_side[...], right_side[:, n4]).astype(BF)
+
+    def bias_grads():
         sums = jnp.sum(bsum[...], axis=0, keepdims=True)
         for n in range(10):
             bias[n : n + 1, :] = sums[:, 128 * n : 128 * n + 128]
@@ -393,14 +462,54 @@
     for c in range(4):
         halo_wait(4 + c)
         chunk(c)
-    weight_grads()
-    reduce_all(g, bias, gout, bout, *ar, hook=local_rest)
+        adjoint_send(SENDS[c])
+    red = make_reduce(g, bias, gout, bout, *ar)
+    weight_grad(0)
+    red["pair"](0)
+    weight_grad(1)
+    red["pair"](1)
+    red["over_first"](0)
+    weight_grad(2)
+    red["pair"](2)
+    bias_grads()
+    red["pair_bias"]()
+    red["over_first"](1)
+    red["over_first"](2)
+    red["bias_first"]()
+    local_rest()
+    write(embed, embed_hbm)
+    for stage in ("over_second", "over_z", "back_z", "back_second", "back_first"):
+        for b in range(3):
+            red[stage](b)
+        adjoint_send(SENDS.get(stage, ()))
+        tail = {"over_second": "bias_second", "over_z": "bias_z", "back_z": "bias_end"}.get(stage)
+        if tail is not None:
+            red[tail]()
     last_sum()
+    write(gradf, gradf_hbm)
+    for b in range(3):
+        red["back_pair"](b)
+    red["back_end"](0)
+    for n in range(4):
+        n4 = slice(256 * n, 256 * n + 256)
+        gwo[n4, :] = gout[0:256, n4].T
+    write(gwo, gwo_hbm)
+    red["back_end"](1)
+    write(gout.at[pl.ds(256, 256), :], gws_hbm)
+    red["back_end"](2)
+    write(gout.at[pl.ds(512, 256), :], gwn_hbm)
+    red["finish"]()
     for c in halo:
         c.wait_send()
+    for c in writes:
+        c.wait()
 
 
 LAYER_SCRATCH = [
+    pltpu.VMEM((1024, 256), BF),
+    pltpu.VMEM((1024, 256), BF),
+    pltpu.VMEM((768, 1024), BF),
+    pltpu.VMEM((1024, 256), BF),
     pltpu.VMEM((3072, 256), BF),
     pltpu.VMEM((16, 64, 512), jnp.int32),
     pltpu.VMEM((256, 1024), BF),
@@ -429,6 +538,7 @@
     pltpu.VMEM((768, 1024), BF),
     pltpu.VMEM((16, 128), F32),
     pltpu.SemaphoreType.DMA((6,)),
+    pltpu.SemaphoreType.DMA((5,)),
     pltpu.SemaphoreType.DMA((16,)),
     pltpu.SemaphoreType.DMA((16,)),
 ]
@@ -440,16 +550,18 @@
     vm = pl.BlockSpec(memory_space=pltpu.VMEM)
     hbm = pl.BlockSpec(memory_space=pl.ANY)
     sm = pl.BlockSpec(memory_space=pltpu.SMEM)
-    embed, grad_features, g, bias = pl.pallas_call(
+    embed, grad_features, gwo, gws, gwn, bias = pl.pallas_call(
         layer_kernel,
         out_shape=(
             jax.ShapeDtypeStruct((1024, 256), BF),
             jax.ShapeDtypeStruct((1024, 256), BF),
-            jax.ShapeDtypeStruct((768, 1024), BF),
+            jax.ShapeDtypeStruct((1024, 256), BF),
+            jax.ShapeDtypeStruct((256, 1024), BF),
+            jax.ShapeDtypeStruct((256, 1024), BF),
             jax.ShapeDtypeStruct((16, 128), F32),
         ),
         in_specs=[sm, hbm, hbm, hbm, hbm, vm, hbm, vm, hbm],
-        out_specs=(vm, vm, vm, vm),
+        out_specs=(hbm, hbm, hbm, hbm, hbm, vm),
         scratch_shapes=LAYER_SCRATCH + AR_SCRATCH,
         compiler_params=pltpu.CompilerParams(
             collective_id=0, has_side_effects=True, vmem_limit_bytes=60 << 20
@@ -460,10 +572,15 @@
         bias_hidden.reshape(1, 1024), w_out, bias_out.reshape(1, 256), cotangent,
     )
     scale = 1.0 / math.sqrt(1024 * 256)
-    g = g.astype(F32) * scale
     bias = bias.reshape(-1) * scale
     return (
-        embed, grad_features, g[:256], g[256:512], bias[:1024], g[512:].T, bias[1024:1280],
+        embed,
+        grad_features,
+        gws.astype(F32) * scale,
+        gwn.astype(F32) * scale,
+        bias[:1024],
+        gwo.astype(F32) * scale,
+        bias[1024:1280],
     )
 
 

time: 92.8 us -> 84.3 us (0.908)
  Pallas kernels: 83.8 us -> 76.8 us
  local copies, waits for them, and re-layouts: 5.59 us -> 2.76 us
  other arithmetic: 2.52 us -> 3.92 us
    pallas_call x1, Pallas kernels: 83.8 us -> 76.8 us  [local(): pl.pallas_call(layer_kernel, out_shape=(jax.ShapeDtypeStruct((1024, 256),...]
    mul x1 -> x2, other arithmetic: 1.82 us -> 3.92 us  [the longest x1 2.88 us: local(): gwn.astype(F32) * scale]
    transpose x1 -> x0, local copies, waits for them, and re-layouts: 1.54 us -> none  [local(): g[512:]]
    unnamed x7 -> x10, local copies, waits for them, and re-layouts: 2.9 us -> 1.6 us
where the time goes in v4:
time: 84.3 us; the launch traced here: 84.2 us
  Pallas kernels  76.8 us (91%)
  other arithmetic  3.92 us (5%)
  local copies, waits for them, and re-layouts  2.76 us (3%)
    pallas_call x1, Pallas kernels, local(): pl.pallas_call(layer_kernel, out_shape=(jax.ShapeDtypeStruct((1024, 256),...  76.8 us
    mul x1, other arithmetic, local(): gwn.astype(F32) * scale  2.88 us

profile of v4, /device:TPU:1, one launch (start us, length us, event | category | flops | bytes accessed | tf_op | source)
XLA Modules:
  0.0 84.2 jit_solution(9139392491994656646)
XLA Ops:
  0.6 76.8 %layer.1 = (bf16[1024,256]{1,0:T(8,128)(2,1)}, bf16[1024,256]{1,0:T(8,128)(2,1)}, bf16[1024,256]{1,0:T(8,128)(2,1)}, bf16[256,1024]{1,0:T(8,128)(2,1)}, bf16[256,1024]{1,0:T(8,128)(2,1)}, /*index=5*/f32[16,128]{1,0:T(8,128)}) custom-call(s32[8,16]{1,0:T(8,128)} %bitcast.7, bf16[1024,256]{1,0:T(8,128)(2,1)} %x_hbm.1, s32[16,64,512]{2,1,0:T(8,128)} %tw_hbm.1, ...), custom_call_target="tpu_custom_call" | custom-call | tf_op jit(solution)/shard_map/layer/pallas_call | solution.py:553
  77.5 0.0 copy-start.3
  77.5 0.0 copy-start
  77.5 0.0 copy-start.2
  77.5 2.9 %convert_multiply_fusion.1 = (f32[256,1024]{1,0:T(8,128)}, f32[256,1024]{1,0:T(8,128)}) fusion(bf16[256,1024]{1,0:T(8,128)(2,1)} %get-tuple-element.16, bf16[256,1024]{1,0:T(8,128)(2,1)} %get-tuple-element.15), kind=kLoop, calls=%fused_computation.1 | loop fusion | flops 1048576 | bytes 3145728 | tf_op jit(solution)/shard_map/mul | solution.py:580
  80.4 0.0 copy-start.1
  80.4 0.0 copy-done.3
  80.4 0.6 slice_bitcast_fusion
  81.0 0.6 slice_bitcast_fusion.1
  81.5 0.0 copy-done
  81.5 1.0 %convert_multiply_fusion = f32[1024,256]{1,0:T(8,128)} fusion(bf16[1024,256]{1,0:T(8,128)(2,1)S(1)} %copy-done), kind=kLoop, calls=%fused_computation | loop fusion | flops 524288 | bytes 1572864 | tf_op jit(solution)/shard_map/mul | solution.py:582
  82.6 0.0 copy-done.2
  82.6 0.8 copy.18
  83.4 0.0 copy-done.1
  83.4 0.8 copy.19
  (1 shorter events, 0.0 us)
Async XLA Ops:
  77.5 2.9 %copy-start.3 = (f32[16,128]{1,0:T(8,128)S(1)}, f32[16,128]{1,0:T(8,128)}, u32[]{:S(2)}) copy-start(f32[16,128]{1,0:T(8,128)} %get-tuple-element.17) | copy-start | bytes 24580
  77.5 4.1 %copy-start = (bf16[1024,256]{1,0:T(8,128)(2,1)S(1)}, bf16[1024,256]{1,0:T(8,128)(2,1)}, u32[]{:S(2)}) copy-start(bf16[1024,256]{1,0:T(8,128)(2,1)} %get-tuple-element.18) | copy-start | bytes 1572868
  77.5 5.1 %copy-start.2 = (bf16[1024,256]{1,0:T(8,128)(2,1)S(1)}, bf16[1024,256]{1,0:T(8,128)(2,1)}, u32[]{:S(2)}) copy-start(bf16[1024,256]{1,0:T(8,128)(2,1)} %get-tuple-element.28) | copy-start | bytes 1572868
  80.4 3.0 %copy-start.1 = (bf16[1024,256]{1,0:T(8,128)(2,1)S(1)}, bf16[1024,256]{1,0:T(8,128)(2,1)}, u32[]{:S(2)}) copy-start(bf16[1024,256]{1,0:T(8,128)(2,1)} %get-tuple-element.29) | copy-start | bytes 1572868

commit v5 on v4

--- a/solution.py
+++ b/solution.py
@@ -405,6 +405,8 @@
                 dh[r, n4] = d
                 bsum[:, n4] += jnp.sum(d.astype(F32).reshape(4, 8, 256), axis=0)
 
+    def adjoint(c):
+        r4 = slice(256 * c, 256 * c + 256)
         da = mm_t(wn[...], dh[r4, :]).astype(BF)
         da_t[c] = da
         for j in range(c, 4):
@@ -459,21 +461,23 @@
     for n in range(4):
         halo_wait(n)
     low_part()
+    red = make_reduce(g, bias, gout, bout, *ar)
     for c in range(4):
         halo_wait(4 + c)
         chunk(c)
+        if c == 3:
+            weight_grad(0)
+            red["pair"](0)
+        adjoint(c)
         adjoint_send(SENDS[c])
-    red = make_reduce(g, bias, gout, bout, *ar)
-    weight_grad(0)
-    red["pair"](0)
+    red["over_first"](0)
     weight_grad(1)
     red["pair"](1)
-    red["over_first"](0)
     weight_grad(2)
     red["pair"](2)
+    red["over_first"](1)
     bias_grads()
     red["pair_bias"]()
-    red["over_first"](1)
     red["over_first"](2)
     red["bias_first"]()
     local_rest()
@@ -544,6 +548,44 @@
 ]
 
 
+def scale_kernel(embed, gradf, gws, gwn, bias, gwo, embed_o, gradf_o, gws_o, gwn_o, bh_o, gwo_o, bo_o):
+    scale = 1.0 / math.sqrt(1024 * 256)
+    embed_o[...] = embed[...]
+    gradf_o[...] = gradf[...]
+    gws_o[...] = gws[...].astype(F32) * scale
+    gwn_o[...] = gwn[...].astype(F32) * scale
+    gwo_o[...] = gwo[...].astype(F32) * scale
+    bh_o[...] = bias[0:8, :] * scale
+    bo_o[...] = bias[8:10, :] * scale
+
+
+def scaled_outputs(embed, gradf, gws, gwn, bias, gwo):
+    steps = 4
+    tall = pl.BlockSpec((1024 // steps, 256), lambda i: (i, 0))
+    wide = pl.BlockSpec((256 // steps, 1024), lambda i: (i, 0))
+
+    def whole(rows):
+        return pl.BlockSpec((rows, 128), lambda i: (0, 0))
+
+    embed, gradf, gws, gwn, bh, gwo, bo = pl.pallas_call(
+        scale_kernel,
+        grid=(steps,),
+        out_shape=(
+            jax.ShapeDtypeStruct((1024, 256), BF),
+            jax.ShapeDtypeStruct((1024, 256), BF),
+            jax.ShapeDtypeStruct((256, 1024), F32),
+            jax.ShapeDtypeStruct((256, 1024), F32),
+            jax.ShapeDtypeStruct((8, 128), F32),
+            jax.ShapeDtypeStruct((1024, 256), F32),
+            jax.ShapeDtypeStruct((2, 128), F32),
+        ),
+        in_specs=[tall, tall, wide, wide, whole(16), tall],
+        out_specs=(tall, tall, wide, wide, whole(8), tall, whole(2)),
+        name="scaled_outputs",
+    )(embed, gradf, gws, gwn, bias, gwo)
+    return embed, gradf, gws, gwn, bh.reshape(1024), gwo, bo.reshape(256)
+
+
 def local(
     node_features, tile_cols, tile_weights, w_self, w_neigh, bias_hidden, w_out, bias_out, cotangent
 ):
@@ -571,17 +613,7 @@
         tile_cols.T, node_features, tile_weights, w_self, w_neigh,
         bias_hidden.reshape(1, 1024), w_out, bias_out.reshape(1, 256), cotangent,
     )
-    scale = 1.0 / math.sqrt(1024 * 256)
-    bias = bias.reshape(-1) * scale
-    return (
-        embed,
-        grad_features,
-        gws.astype(F32) * scale,
-        gwn.astype(F32) * scale,
-        bias[:1024],
-        gwo.astype(F32) * scale,
-        bias[1024:1280],
-    )
+    return scaled_outputs(embed, grad_features, gws, gwn, bias, gwo)
 
 
 def solution(mesh):

time: 84.3 us -> 81.6 us (0.968)
  Pallas kernels: 76.8 us -> 80.8 us
  other arithmetic: 3.92 us -> 0 us
  local copies, waits for them, and re-layouts: 2.76 us -> 0 us
    pallas_call x0 -> x1, Pallas kernels: none -> 4.33 us  [scaled_outputs(): pl.pallas_call(scale_kernel, grid=(steps,), out_shape=(jax.ShapeDtypeStru...]
    mul x3 -> x0, other arithmetic: 3.92 us -> none  [the longest x1 2.88 us: local(): gwn.astype(F32) * scale]
    unnamed x10 -> x0, local copies, waits for them, and re-layouts: 1.6 us -> none
    slice x2 -> x0, local copies, waits for them, and re-layouts: 1.16 us -> none  [the longest x1 0.6 us: local(): bias[:1024]]
where the time goes in v5:
time: 81.6 us; the launch traced here: 81.5 us
  Pallas kernels  80.8 us (99%)
    pallas_call x1, Pallas kernels, local(): pl.pallas_call(layer_kernel, out_shape=(jax.ShapeDtypeStruct((1024, 256),...  76.5 us
    pallas_call x1, Pallas kernels, scaled_outputs(): pl.pallas_call(scale_kernel, grid=(steps,), out_shape=(jax.ShapeDtypeStru...  4.33 us

profile of v5, /device:TPU:1, one launch (start us, length us, event | category | flops | bytes accessed | tf_op | source)
XLA Modules:
  0.0 81.5 jit_solution(17096959124185649918)
XLA Ops:
  0.6 76.5 %layer.1 = (bf16[1024,256]{1,0:T(8,128)(2,1)}, bf16[1024,256]{1,0:T(8,128)(2,1)}, bf16[1024,256]{1,0:T(8,128)(2,1)}, bf16[256,1024]{1,0:T(8,128)(2,1)}, bf16[256,1024]{1,0:T(8,128)(2,1)}, /*index=5*/f32[16,128]{1,0:T(8,128)}) custom-call(s32[8,16]{1,0:T(8,128)} %bitcast.5, bf16[1024,256]{1,0:T(8,128)(2,1)} %x_hbm.1, s32[16,64,512]{2,1,0:T(8,128)} %tw_hbm.1, ...), custom_call_target="tpu_custom_call" | custom-call | tf_op jit(solution)/shard_map/layer/pallas_call | solution.py:595
  77.1 4.3 %scaled_outputs.1 = (bf16[1024,256]{1,0:T(8,128)(2,1)}, bf16[1024,256]{1,0:T(8,128)(2,1)}, f32[256,1024]{1,0:T(8,128)}, f32[256,1024]{1,0:T(8,128)}, f32[8,128]{...) custom-call(bf16[1024,256]{1,0:T(8,128)(2,1)} %get-tuple-element.20.embed, ...), custom_call_target="tpu_custom_call" | custom-call | tf_op jit(solution)/shard_map/scaled_outputs/pallas_call | solution.py:570

commit v6 on v5

--- a/solution.py
+++ b/solution.py
@@ -55,6 +55,7 @@
     first = ((xs, x), (ys, y))
     second = ((ys, y), (xs, x))
     sent = []
+    drained = [0]
 
     def go(src, dst, rsem, dev):
         c = remote(src, dst, send.at[len(sent)], recv.at[rsem], dev)
@@ -204,14 +205,22 @@
             for j in range(4):
                 land(gout.at[part(b, h, j), other], n_coreback(b, h, j))
 
+    def drain(count):
+        for c in sent[drained[0] : count]:
+            c.wait_send()
+        drained[0] = max(count, drained[0])
+
     def finish():
-        for c in sent:
-            c.wait_send()
+        drain(len(sent))
+
+    def started():
+        return len(sent)
 
     return dict(pair=pair, pair_bias=pair_bias, over_first=over_first, bias_first=bias_first,
                 over_second=over_second, bias_second=bias_second, over_z=over_z, bias_z=bias_z,
                 back_z=back_z, bias_end=bias_end, back_second=back_second, back_first=back_first,
-                back_pair=back_pair, back_end=back_end, finish=finish)
+                back_pair=back_pair, back_end=back_end, finish=finish,
+                drain=drain, started=started)
 
 
 AR_SCRATCH = [
@@ -259,6 +268,8 @@
 
 SENDS = {0: (0,), 1: (1,), 2: (2,), 3: (7, 3, 6), "back_z": (5, 4)}
 
+REST = {"over_z": (0, 4)}
+
 
 def neighbours():
     row, z_lo, core, x, y, z = coords()
@@ -303,15 +314,19 @@
         halo.append(c)
 
     def halo_wait(n):
-        dst = win.at[pl.ds(256 * n if n < 4 else 1024 + 256 * n, 256), :]
+        first, size = (256 * n, 256)
+        for f, size_f, n_f in highs:
+            if n_f == n:
+                first, size = 2048 + f, size_f
+        dst = win.at[pl.ds(first, size), :]
         remote(dst, dst, halo_send.at[n], halo_recv.at[n], left).wait_recv()
 
     for i in range(4):
         rows = pl.ds(256 * i, 256)
         halo_copy(x_hbm.at[rows, :], win.at[rows, :], i, right)
-    for i in range(4):
-        rows = pl.ds(256 * i, 256)
-        halo_copy(x_hbm.at[rows, :], win.at[pl.ds(2048 + 256 * i, 256), :], 4 + i, left)
+    highs = ((0, 256, 4), (256, 256, 5), (512, 256, 6), (768, 128, 7), (896, 128, 16))
+    for first, size, n in highs:
+        halo_copy(x_hbm.at[pl.ds(first, size), :], win.at[pl.ds(2048 + first, size), :], n, left)
 
     def build_dense():
         lane = lax.broadcasted_iota(jnp.int32, (64, 128), 1)
@@ -378,21 +393,22 @@
             buf, dst, dev = ((lo_b, from_r, left), (hi_b, from_l, right))[n // 4]
             halo_copy(buf.at[j], dst.at[j], 8 + n, dev)
 
-    def chunk(c):
-        r4 = slice(256 * c, 256 * c + 256)
+    def chunk(c, top=0, m=256, last=256):
+        r4 = slice(256 * c + top, 256 * c + top + m)
         total = agg0[r4, :]
         for t in range(c + 1):
             b = 256 * (8 + t - c)
-            total = total + mm(dense[c, :, b : b + 256], win[2048 + 256 * t : 2304 + 256 * t, :])
+            k = last if t == c else 256
+            total = total + mm(dense[c, top : top + m, b : b + k], win[2048 + 256 * t : 2048 + 256 * t + k, :])
         ag = total.astype(BF)
         for n in range(4):
             n4 = slice(256 * n, 256 * n + 256)
             pre[r4, n4] += mm(ag, wn[:, n4])
         at[:, r4] = ag.T
 
-        @pl.loop(0, 8)
+        @pl.loop(0, m // 32)
         def _(i):
-            r = pl.ds(pl.multiple_of(c * 256 + i * 32, 32), 32)
+            r = pl.ds(pl.multiple_of(c * 256 + top + i * 32, 32), 32)
             for n in range(4):
                 n4 = slice(256 * n, 256 * n + 256)
                 v = pre[r, n4]
@@ -435,8 +451,8 @@
             bias[n : n + 1, :] = sums[:, 128 * n : 128 * n + 128]
         bias[10:16, :] = jnp.zeros((6, 128), F32)
 
-    def local_rest():
-        @pl.loop(0, 4)
+    def local_rest(first, last):
+        @pl.loop(first, last)
         def _(c):
             rows = ds256(c)
             embed[rows, :] = (mm(hid[rows, :], wo[...]) + bo[...]).astype(BF)
@@ -464,8 +480,12 @@
     red = make_reduce(g, bias, gout, bout, *ar)
     for c in range(4):
         halo_wait(4 + c)
-        chunk(c)
-        if c == 3:
+        if c < 3:
+            chunk(c)
+        else:
+            chunk(c, 0, 128, 128)
+            halo_wait(16)
+            chunk(c, 128, 128, 256)
             weight_grad(0)
             red["pair"](0)
         adjoint(c)
@@ -480,24 +500,31 @@
     red["pair_bias"]()
     red["over_first"](2)
     red["bias_first"]()
-    local_rest()
-    write(embed, embed_hbm)
     for stage in ("over_second", "over_z", "back_z", "back_second", "back_first"):
+        before = red["started"]()
         for b in range(3):
             red[stage](b)
         adjoint_send(SENDS.get(stage, ()))
+        if stage in REST:
+            local_rest(*REST[stage])
+            if REST[stage][1] == 4:
+                write(embed, embed_hbm)
         tail = {"over_second": "bias_second", "over_z": "bias_z", "back_z": "bias_end"}.get(stage)
         if tail is not None:
             red[tail]()
+        red["drain"](before)
     last_sum()
     write(gradf, gradf_hbm)
-    for b in range(3):
-        red["back_pair"](b)
+    before = red["started"]()
+    red["back_pair"](0)
+    red["back_pair"](1)
     red["back_end"](0)
     for n in range(4):
         n4 = slice(256 * n, 256 * n + 256)
         gwo[n4, :] = gout[0:256, n4].T
     write(gwo, gwo_hbm)
+    red["back_pair"](2)
+    red["drain"](before)
     red["back_end"](1)
     write(gout.at[pl.ds(256, 256), :], gws_hbm)
     red["back_end"](2)
@@ -543,8 +570,8 @@
     pltpu.VMEM((16, 128), F32),
     pltpu.SemaphoreType.DMA((6,)),
     pltpu.SemaphoreType.DMA((5,)),
-    pltpu.SemaphoreType.DMA((16,)),
-    pltpu.SemaphoreType.DMA((16,)),
+    pltpu.SemaphoreType.DMA((17,)),
+    pltpu.SemaphoreType.DMA((17,)),
 ]
 
 
@@ -560,7 +587,7 @@
 
 
 def scaled_outputs(embed, gradf, gws, gwn, bias, gwo):
-    steps = 4
+    steps = 2
     tall = pl.BlockSpec((1024 // steps, 256), lambda i: (i, 0))
     wide = pl.BlockSpec((256 // steps, 1024), lambda i: (i, 0))
 

time: 81.6 us -> 81.1 us (level)
    pallas_call x1, Pallas kernels: 4.33 us -> 3.44 us  [scaled_outputs(): pl.pallas_call(scale_kernel, grid=(steps,), out_shape=(jax.ShapeDtypeStru...]
where the time goes in v6:
time: 81.1 us; the launch traced here: 80.9 us
  Pallas kernels  80.3 us (99%)
    pallas_call x1, Pallas kernels, local(): pl.pallas_call(layer_kernel, out_shape=(jax.ShapeDtypeStruct((1024, 256),...  76.9 us
    pallas_call x1, Pallas kernels, scaled_outputs(): pl.pallas_call(scale_kernel, grid=(steps,), out_shape=(jax.ShapeDtypeStru...  3.44 us

profile of v6, /device:TPU:1, one launch (start us, length us, event | category | flops | bytes accessed | tf_op | source)
XLA Modules:
  0.0 80.9 jit_solution(13175321212742812074)
XLA Ops:
  0.6 76.9 %layer.1 = (bf16[1024,256]{1,0:T(8,128)(2,1)}, bf16[1024,256]{1,0:T(8,128)(2,1)}, bf16[1024,256]{1,0:T(8,128)(2,1)}, bf16[256,1024]{1,0:T(8,128)(2,1)}, bf16[256,1024]{1,0:T(8,128)(2,1)}, /*index=5*/f32[16,128]{1,0:T(8,128)}) custom-call(s32[8,16]{1,0:T(8,128)} %bitcast.5, bf16[1024,256]{1,0:T(8,128)(2,1)} %x_hbm.1, s32[16,64,512]{2,1,0:T(8,128)} %tw_hbm.1, ...), custom_call_target="tpu_custom_call" | custom-call | tf_op jit(solution)/shard_map/layer/pallas_call | solution.py:622
  77.5 3.4 %scaled_outputs.1 = (bf16[1024,256]{1,0:T(8,128)(2,1)}, bf16[1024,256]{1,0:T(8,128)(2,1)}, f32[256,1024]{1,0:T(8,128)}, f32[256,1024]{1,0:T(8,128)}, f32[8,128]{...) custom-call(bf16[1024,256]{1,0:T(8,128)(2,1)} %get-tuple-element.20.embed, ...), custom_call_target="tpu_custom_call" | custom-call | tf_op jit(solution)/shard_map/scaled_outputs/pallas_call | solution.py:597

commit v7 on v6

--- a/solution.py
+++ b/solution.py
@@ -488,11 +488,11 @@
             chunk(c, 128, 128, 256)
             weight_grad(0)
             red["pair"](0)
+            weight_grad(1)
+            red["pair"](1)
+            red["over_first"](0)
         adjoint(c)
         adjoint_send(SENDS[c])
-    red["over_first"](0)
-    weight_grad(1)
-    red["pair"](1)
     weight_grad(2)
     red["pair"](2)
     red["over_first"](1)

time: 81.1 us -> 81.3 us (level)
  no operation moved by 1% of the time
where the time goes in v7:
time: 81.3 us; the launch traced here: 81.1 us
  Pallas kernels  80.5 us (99%)
    pallas_call x1, Pallas kernels, local(): pl.pallas_call(layer_kernel, out_shape=(jax.ShapeDtypeStruct((1024, 256),...  77.1 us
    pallas_call x1, Pallas kernels, scaled_outputs(): pl.pallas_call(scale_kernel, grid=(steps,), out_shape=(jax.ShapeDtypeStru...  3.44 us

profile of v7, /device:TPU:1, one launch (start us, length us, event | category | flops | bytes accessed | tf_op | source)
XLA Modules:
  0.0 81.1 jit_solution(13986879162388076317)
XLA Ops:
  0.6 77.1 %layer.1 = (bf16[1024,256]{1,0:T(8,128)(2,1)}, bf16[1024,256]{1,0:T(8,128)(2,1)}, bf16[1024,256]{1,0:T(8,128)(2,1)}, bf16[256,1024]{1,0:T(8,128)(2,1)}, bf16[256,1024]{1,0:T(8,128)(2,1)}, /*index=5*/f32[16,128]{1,0:T(8,128)}) custom-call(s32[8,16]{1,0:T(8,128)} %bitcast.5, bf16[1024,256]{1,0:T(8,128)(2,1)} %x_hbm.1, s32[16,64,512]{2,1,0:T(8,128)} %tw_hbm.1, ...), custom_call_target="tpu_custom_call" | custom-call | tf_op jit(solution)/shard_map/layer/pallas_call | solution.py:622
  77.7 3.4 %scaled_outputs.1 = (bf16[1024,256]{1,0:T(8,128)(2,1)}, bf16[1024,256]{1,0:T(8,128)(2,1)}, f32[256,1024]{1,0:T(8,128)}, f32[256,1024]{1,0:T(8,128)}, f32[8,128]{...) custom-call(bf16[1024,256]{1,0:T(8,128)(2,1)} %get-tuple-element.20.embed, ...), custom_call_target="tpu_custom_call" | custom-call | tf_op jit(solution)/shard_map/scaled_outputs/pallas_call | solution.py:597
